TPU v7x, 128 devices: a whole 4x4x4 slice. The times are simulated.
128 devices in a mesh: cache: 32 (over y, z, core), mp: 4 (over x).
Axes of the slice: x: 4, y: 4, z: 4, core: 2. Of those that a mesh axis runs over, the one named last changes fastest.
Arguments:
- tokens: bfloat16 [262144, 768], P(('cache', 'mp')), may hold values from -6 to 6
- w_in: bfloat16 [768, 3072], P(None, 'mp'), may hold values from -0.21875 to 0.21875
- w_out: bfloat16 [3072, 768], P('mp'), may hold values from -0.109375 to 0.109375
- gain_in: float32 [768], replicated, may hold values from 0.1 to 1.9
- gain_out: float32 [768], replicated, may hold values from 0.1 to 1.9
- stale_cache: bfloat16 [131072, 768], P(('cache', 'mp')), may hold values from -6 to 6
- refresh_ids: int32 [4096], P(('cache', 'mp')), may hold values from 0 to 131071, as said below
- queries: bfloat16 [16384, 768], P(('cache', 'mp')), may hold values from -110 to 110
- neg_blocks: int32 [16384, 8], P(('cache', 'mp')), may hold values from 0 to 1023, all different within a row; in each aligned block of 128 rows (0 to 127, 128 to 255, ...) at most 2 rows name the same one
- positive_ids: int32 [16384], P(('cache', 'mp')), may hold values from 0 to 31
Outputs:
- new_cache: bfloat16 [131072, 768], P(('cache', 'mp'))
- loss: float32 [16384], P(('cache', 'mp'))
- query_grad: float32 [16384, 768], P(('cache', 'mp'))
Inputs may be any that keep to these rules, and one draw needn't show every extreme that they name: `refresh_ids`: all ids differ. The documents of one device name at most 2 rows within any one range of 4096 rows that one index of cache holds, and in every draw one such range receives exactly 2 rows from every device. `neg_blocks`: each query lists 8 different blocks. The queries of one device list one block at most 2 times, and some block exactly that often.
All inputs are finite; a program needn't handle non-finite values.
Results may differ from a plain program's by a relative error of at most 0.0034.
Values may be sent and summed in bfloat16 or wider, within the bound.
A program may use at most 128 MiB of HBM per device.

v0:
```python
import jax
import jax.numpy as jnp
from jax import lax
from jax.sharding import Mesh, PartitionSpec as P

D = 768
BLOCK = 128


epsilon = 1e-06
CACHE = ("chip", "core")


def norm_rows(values):
    values = values.astype(jnp.float32)
    return values * lax.rsqrt(jnp.mean(values * values, axis=-1, keepdims=True) + epsilon)


def shards(
    tokens,
    w_in,
    w_out,
    gain_in,
    gain_out,
    stale_cache,
    refresh_ids,
    queries,
    neg_blocks,
    positive_ids,
):
    cache_count = lax.axis_size(CACHE)
    mp_count = lax.axis_size("mp")
    docs_here = refresh_ids.shape[0]
    tok_rows = tokens.shape[0]
    doc_len = tok_rows // docs_here
    width = tokens.shape[1]
    logit_scale = D ** (-0.5)
    normed = (norm_rows(tokens) * gain_in).astype(jnp.bfloat16)
    piece_count = cache_count
    piece_rows = w_out.shape[0] // piece_count
    piece_at = lax.axis_index(CACHE) * piece_rows
    own_piece = lax.dynamic_slice_in_dim(w_out, piece_at, piece_rows, axis=0)
    mp_pieces = lax.all_to_all(
        jnp.broadcast_to(own_piece[None], (mp_count,) + own_piece.shape),
        "mp",
        split_axis=0,
        concat_axis=0,
        tiled=True,
    )
    all_pieces = lax.all_to_all(
        jnp.broadcast_to(mp_pieces[None], (piece_count,) + mp_pieces.shape),
        CACHE,
        split_axis=0,
        concat_axis=0,
        tiled=True,
    )
    w_out_full = jnp.transpose(all_pieces, (1, 0, 2, 3)).reshape(-1, width)
    hidden = jnp.maximum(
        jnp.dot(
            normed,
            lax.all_gather(w_in, "mp", axis=1, tiled=True),
            preferred_element_type=jnp.float32,
        ),
        0.0,
    ).astype(jnp.bfloat16)
    mixed = jnp.dot(hidden, w_out_full, preferred_element_type=jnp.float32)
    state_sum = tokens.astype(jnp.float32) + mixed
    final_rows = norm_rows(state_sum) * gain_out
    pooled = jnp.mean(final_rows.reshape(docs_here, doc_len, width), axis=1)
    embedded = norm_rows(pooled).astype(jnp.bfloat16)
    rows_own = stale_cache.shape[0]
    group_rows = rows_own * mp_count
    refresh_cap = 2 * docs_here // cache_count
    group_of = refresh_ids // group_rows
    group_hits = (group_of[:, None] == jnp.arange(cache_count, dtype=jnp.int32)[None, :]).astype(
        jnp.int32
    )
    rank_in = jnp.sum(group_hits * (jnp.cumsum(group_hits, axis=0) - 1), axis=1)
    slot_of = group_of * refresh_cap + rank_in
    filled = (
        jnp.full((cache_count * refresh_cap,), -1, jnp.int32)
        .at[slot_of]
        .set(jnp.arange(docs_here, dtype=jnp.int32))
    )
    slot_used = filled >= 0
    slot_doc = jnp.maximum(filled, 0)
    out_rows = jnp.where(slot_used[:, None], embedded[slot_doc], jnp.zeros((), jnp.bfloat16))
    out_ids = jnp.where(slot_used, refresh_ids[slot_doc], -1)
    got_rows, got_ids = (
        lax.all_to_all(out_rows, CACHE, split_axis=0, concat_axis=0, tiled=True),
        lax.all_to_all(out_ids, CACHE, split_axis=0, concat_axis=0, tiled=True),
    )
    all_rows, all_ids = (
        lax.all_gather(got_rows, "mp", axis=0, tiled=True),
        lax.all_gather(got_ids, "mp", axis=0, tiled=True),
    )
    row_base = (lax.axis_index(CACHE) * mp_count + lax.axis_index("mp")) * rows_own
    local_row = all_ids - row_base
    write_table = jnp.arange(rows_own, dtype=jnp.int32)[:, None] == local_row[None, :]
    placed = jnp.dot(
        write_table.astype(jnp.bfloat16), all_rows, preferred_element_type=jnp.float32
    ).astype(jnp.bfloat16)
    written = jnp.any(write_table, axis=1)
    fresh_cache = jnp.where(written[:, None], placed, stale_cache)
    local_blocks = rows_own // BLOCK
    device_count = cache_count * mp_count
    block_count = local_blocks * device_count
    query_count, neg_count = neg_blocks.shape
    pair_count = query_count * neg_count
    query_cap = max(2, 2 * pair_count // block_count)
    pair_blocks = neg_blocks.reshape(-1)
    pair_marks = (pair_blocks[:, None] == jnp.arange(block_count, dtype=jnp.int32)[None, :]).astype(
        jnp.int32
    )
    pair_rank = jnp.sum(pair_marks * (jnp.cumsum(pair_marks, axis=0) - 1), axis=1)
    pair_slots = pair_blocks * query_cap + pair_rank
    slot_pair = (
        jnp.full((block_count * query_cap,), -1, jnp.int32)
        .at[pair_slots]
        .set(jnp.arange(pair_count, dtype=jnp.int32))
    )
    outbound = jnp.where(
        (slot_pair >= 0)[:, None],
        queries[jnp.maximum(slot_pair, 0) // neg_count],
        jnp.zeros((), jnp.bfloat16),
    )
    arrived = lax.all_to_all(outbound, CACHE + ("mp",), split_axis=0, concat_axis=0, tiled=True)
    arrived = arrived.reshape(device_count, local_blocks, query_cap, width)
    block_keys = fresh_cache.reshape(local_blocks, BLOCK, width)
    scores = (
        jnp.einsum("snkd,nrd->snkr", arrived, block_keys, preferred_element_type=jnp.float32)
        * logit_scale
    )
    block_peak = jnp.max(scores, axis=-1)
    exp_terms = jnp.exp(scores - block_peak[..., None])
    block_total = jnp.sum(exp_terms, axis=-1)
    weights = exp_terms.astype(jnp.bfloat16)
    mixture = jnp.einsum("snkr,nrd->snkd", weights, block_keys, preferred_element_type=jnp.float32)
    back_mix, back_peak, back_total = (
        lax.all_to_all(
            mixture.reshape(-1, width), CACHE + ("mp",), split_axis=0, concat_axis=0, tiled=True
        ),
        lax.all_to_all(
            block_peak.reshape(-1), CACHE + ("mp",), split_axis=0, concat_axis=0, tiled=True
        ),
        lax.all_to_all(
            block_total.reshape(-1), CACHE + ("mp",), split_axis=0, concat_axis=0, tiled=True
        ),
    )
    pair_mix = back_mix[pair_slots].reshape(query_count, neg_count, width)
    pair_peak = back_peak[pair_slots].reshape(query_count, neg_count)
    pair_total = back_total[pair_slots].reshape(query_count, neg_count)
    pick_table = (positive_ids[:, None] == jnp.arange(docs_here, dtype=jnp.int32)[None, :]).astype(
        jnp.bfloat16
    )
    positive = jnp.dot(pick_table, embedded, preferred_element_type=jnp.float32).astype(
        jnp.bfloat16
    )
    positive_f = positive.astype(jnp.float32)
    positive_logit = jnp.sum(queries.astype(jnp.float32) * positive_f, axis=-1) * logit_scale
    top_value = jnp.maximum(jnp.max(pair_peak, axis=-1), positive_logit)
    block_weight = jnp.exp(pair_peak - top_value[:, None])
    positive_weight = jnp.exp(positive_logit - top_value)
    partition = jnp.sum(block_weight * pair_total, axis=-1) + positive_weight
    loss = top_value + jnp.log(partition) - positive_logit
    pulled = (
        jnp.einsum("qn,qnd->qd", block_weight, pair_mix) + positive_weight[:, None] * positive_f
    )
    query_grad = logit_scale * (pulled / partition[:, None] - positive_f)
    return (fresh_cache, loss, query_grad)


def solution(mesh):
    placed = (
        P(CACHE + ("mp",), None),
        P(None, "mp"),
        P("mp", None),
        P(),
        P(),
        P(CACHE + ("mp",), None),
        P(CACHE + ("mp",)),
        P(CACHE + ("mp",), None),
        P(CACHE + ("mp",), None),
        P(CACHE + ("mp",)),
    )
    core_count = 2
    split_mesh = Mesh(
        mesh.devices.reshape(mesh.shape["cache"] // core_count, core_count, mesh.shape["mp"]),
        ("chip", "core", "mp"),
    )
    return jax.shard_map(
        shards,
        mesh=split_mesh,
        in_specs=placed,
        out_specs=(P(CACHE + ("mp",), None), P(CACHE + ("mp",)), P(CACHE + ("mp",), None)),
        check_vma=False,
    )
```

profile of v0, /device:TPU:1, one launch (start us, length us, event | category | flops | bytes accessed | tf_op | source)
XLA Modules:
  0.0 281.0 jit_solution(17390284597438780783)
XLA Ops:
  12.4 9.6 %all-to-all-start = ((s32[32,2,1]{1,2,0:T(1,128)}), s32[32,2,1]{1,2,0:T(1,128)S(1)}, u32[]{:S(2)}, u32[]{:S(2)}) async-start(s32[32,2,1]{1,2,0:T(1,128)} %bitcast), calls=%async_computation | async-start | bytes 32768 | tf_op jit(solution)/shard_map/all_to_all | solution.py:91
  22.1 6.9 %all-to-all-done = s32[32,2,1]{1,2,0:T(1,128)S(1)} async-done(((s32[32,2,1]{1,2,0:T(1,128)}), s32[32,2,1]{1,2,0:T(1,128)S(1)}, u32[]{:S(2)}, u32[]{:S(2)}) %all-to-all-start) | async-done | bytes 288 | tf_op jit(solution)/shard_map/all_to_all | solution.py:91
  28.9 11.1 %all_to_all.73 = bf16[4,24,768]{2,1,0:T(8,128)(2,1)S(1)} all-to-all(bf16[4,24,768]{2,1,0:T(8,128)(2,1)S(1)} %broadcast_in_dim.58), channel_id=1, replica_groups=mesh['chip'=16,'core'=2,'mp'=4] {'mp'}, dimensions={0} | all-to-all | bytes 294912 | tf_op jit(solution)/shard_map/all_to_all | solution.py:43
  42.8 6.2 %all-to-all-start.2 = ((bf16[32,4,24,768]{3,2,1,0:T(8,128)(2,1)}), bf16[32,4,24,768]{3,2,1,0:T(8,128)(2,1)}, u32[]{:S(2)}, u32[]{:S(2)}) async-start(bf16[32,4,24,768]{3,2,1,0:T(8,128)(2,1)} %broadcast_in_dim.59), calls=%async_computation.2 | async-start | bytes 9437184 | tf_op jit(solution)/shard_map/all_to_all | solution.py:50
  54.8 4.4 %copy.60 = s32[1024,8,128]{0,2,1:T(8,128)} copy(s32[1024,8,128]{0,1,2:T(8,128)S(1)} %add_add_fusion) | data formatting | bytes 8388608 | tf_op jit(solution)/shard_map/sub | solution.py:115
  62.4 4.3 %scatter_custom_fusion.1 = s32[2048]{0:T(1024)S(1)} fusion(s32[1024]{0:T(1024)S(1)} %bitcast.69, s32[1024]{0:T(1024)S(1)} %iota.25, s32[]{:T(128)} %constant.36.clone.1), kind=kCustom, calls=%fused_computation.73 | custom fusion | bytes 8196 | tf_op jit(solution)/shard_map/scatter | solution.py:120
  68.1 9.4 %gather_fusion.2 = bf16[2048,768]{1,0:T(8,128)(2,1)} fusion(bf16[128,768]{1,0:T(8,128)(2,1)S(1)} %copy-done.2, s32[2048]{0:T(1024)S(1)} %fusion.30), kind=kCustom, calls=%fused_computation.2 | custom fusion | bytes 6299648 | tf_op jit(solution)/shard_map/gather | solution.py:124
  83.8 5.7 %all-reduce = s32[256]{0:T(256)S(1)} all-reduce(s32[256]{0:T(256)S(1)} %dynamic-update-slice), channel_id=1, replica_groups=mesh['chip'=16,'core'=2,'mp'=4] {'mp'}, use_global_device_ids=true, to_apply=%add | all-reduce | flops 256 | bytes 2048
  89.5 17.9 %all-to-all-done.2 = bf16[32,4,24,768]{3,2,1,0:T(8,128)(2,1)} async-done(((bf16[32,4,24,768]{3,2,1,0:T(8,128)(2,1)}), bf16[32,4,24,768]{3,2,1,0:T(8,128)(2,1)}, u32[]{:S(2)}, u32[]{:S(2)}) %all-to-all-start.2) | async-done | bytes 4718624 | tf_op jit(solution)/shard_map/all_to_all | solution.py:50
  107.4 7.8 %all-to-all-start.4 = ((bf16[128,16,768]{2,1,0:T(8,128)(2,1)}), bf16[128,16,768]{2,1,0:T(8,128)(2,1)}, u32[]{:S(2)}, u32[]{:S(2)}) async-start(bf16[128,16,768]{2,1,0:T(8,128)(2,1)} %broadcast_select_fusion), calls=%async_computation.4 | async-start | bytes 6291456 | tf_op jit(solution)/shard_map/all_to_all | solution.py:127
  115.3 4.9 %copy.55 = bf16[32,4,24,768]{3,2,0,1:T(8,128)(2,1)} copy(bf16[32,4,24,768]{3,2,1,0:T(8,128)(2,1)} %all-to-all-done.2) | data formatting | bytes 9437184 | tf_op jit(solution)/shard_map/all_to_all | solution.py:50
  120.2 26.7 %multiply_reduce_fusion = (f32[2048]{0:T(1024)S(1)}, f32[2048,768]{1,0:T(8,128)}) fusion(bf16[2048,768]{1,0:T(8,128)(2,1)} %param.10, bf16[3072,768]{1,0:T(8,128)(2,1)} %bitcast.65, bf16[768,3072]{1,0:T(8,128)(2,1)} %all-gather.2.cloned.1.call-done, f32[768]{0:T(1024)S(1)} %copy-done.11, f32[2048]{0:T(1024)S(1)} %add_rsqrt_fusion.1), kind=kOutput, calls=%fused_computation.17 | convolution fusion | flops 19352516608 | bytes 18893824 | tf_op jit(solution)/shard_map/dot_general | solution.py:66
  146.9 4.4 %bitcast_reduce_fusion = f32[32,768]{1,0:T(8,128)S(1)} fusion(f32[2048,768]{1,0:T(8,128)} %get-tuple-element.9, bf16[2048,768]{1,0:T(8,128)(2,1)} %param.10, f32[768]{0:T(1024)S(1)} %copy-done.8, f32[2048]{0:T(1024)S(1)} %add_rsqrt_fusion), kind=kLoop, calls=%fused_computation.15 | loop fusion | flops 7839744 | bytes 9546752 | tf_op jit(solution)/shard_map/reduce_sum | solution.py:69
  153.0 4.1 %all-to-all-done.4 = bf16[128,16,768]{2,1,0:T(8,128)(2,1)} async-done(((bf16[128,16,768]{2,1,0:T(8,128)(2,1)}), bf16[128,16,768]{2,1,0:T(8,128)(2,1)}, u32[]{:S(2)}, u32[]{:S(2)}) %all-to-all-start.4) | async-done | bytes 3145760 | tf_op jit(solution)/shard_map/all_to_all | solution.py:127
  161.2 4.6 %copy.61 = bf16[128,16,768]{2,0,1:T(8,128)(2,1)} copy(bf16[128,16,768]{2,1,0:T(8,128)(2,1)} %all-to-all-done.4) | data formatting | bytes 6291456 | tf_op jit(solution)/shard_map/all_to_all | solution.py:127
  168.5 11.0 %all_gather.11 = bf16[256,768]{1,0:T(8,128)(2,1)S(1)} all-gather(bf16[64,768]{1,0:T(8,128)(2,1)S(1)} %all_to_all.54), channel_id=1, replica_groups=mesh['chip'=16,'core'=2,'mp'=4] {'mp'}, dimensions={0}, use_global_device_ids=true | all-gather | bytes 491520 | tf_op jit(solution)/shard_map/all_gather | solution.py:94
  182.1 8.6 %all-to-all-start.5 = ((f32[128,16,1]{1,2,0:T(1,128)}), f32[128,16,1]{1,2,0:T(1,128)S(1)}, u32[]{:S(2)}, u32[]{:S(2)}) async-start(f32[128,16,1]{1,2,0:T(1,128)} %copy.62), calls=%async_computation.5 | async-start | bytes 131072 | tf_op jit(solution)/shard_map/all_to_all | solution.py:143
  191.6 9.0 %all-to-all-done.5 = f32[128,16,1]{1,2,0:T(1,128)S(1)} async-done(((f32[128,16,1]{1,2,0:T(1,128)}), f32[128,16,1]{1,2,0:T(1,128)S(1)}, u32[]{:S(2)}, u32[]{:S(2)}) %all-to-all-start.5) | async-done | bytes 8224 | tf_op jit(solution)/shard_map/all_to_all | solution.py:143
  208.7 5.1 %copy.66 = bf16[128,16,768]{2,1,0:T(8,128)(2,1)} copy(bf16[128,16,768]{0,2,1:T(8,128)(2,1)} %bitcast.61) | data formatting | bytes 6291456 | tf_op jit(solution)/shard_map/all_to_all | solution.py:140
  214.5 9.5 %all-to-all-start.7 = ((bf16[128,16,768]{2,1,0:T(8,128)(2,1)}), bf16[128,16,768]{2,1,0:T(8,128)(2,1)}, u32[]{:S(2)}, u32[]{:S(2)}) async-start(bf16[128,16,768]{2,1,0:T(8,128)(2,1)} %copy.66), calls=%async_computation.7 | async-start | bytes 6291456 | tf_op jit(solution)/shard_map/all_to_all | solution.py:140
  225.7 6.1 %gather_fusion.3 = f32[1024]{0:T(1024)S(1)} fusion(f32[2048]{0:T(1024)S(1)} %all_to_all.58, s32[1024]{0:T(1024)S(1)} %broadcast_clamp_fusion), kind=kCustom, calls=%fused_computation.3 | custom fusion | bytes 12288 | tf_op jit(solution)/shard_map/gather | solution.py:151
  232.9 6.1 %gather_fusion.4 = f32[1024]{0:T(1024)S(1)} fusion(f32[2048]{0:T(1024)S(1)} %all_to_all.61, s32[1024]{0:T(1024)S(1)} %broadcast_clamp_fusion), kind=kCustom, calls=%fused_computation.4 | custom fusion | bytes 12288 | tf_op jit(solution)/shard_map/gather | solution.py:152
  240.0 25.9 %all-to-all-done.7 = bf16[128,16,768]{2,1,0:T(8,128)(2,1)} async-done(((bf16[128,16,768]{2,1,0:T(8,128)(2,1)}), bf16[128,16,768]{2,1,0:T(8,128)(2,1)}, u32[]{:S(2)}, u32[]{:S(2)}) %all-to-all-start.7) | async-done | bytes 3145760 | tf_op jit(solution)/shard_map/all_to_all | solution.py:140
  265.9 6.9 %gather_fusion.5 = bf16[1024,768]{1,0:T(8,128)(2,1)S(1)} fusion(bf16[2048,768]{1,0:T(8,128)(2,1)} %bitcast.23, s32[1024]{0:T(1024)S(1)} %broadcast_clamp_fusion), kind=kCustom, calls=%fused_computation.5 | custom fusion | bytes 3149824 | tf_op jit(solution)/shard_map/gather | solution.py:150
  (108 shorter events, 49.8 us)
Async XLA Ops:
  7.2 14.9 %copy-start = (bf16[768,768]{1,0:T(8,128)(2,1)S(1)}, bf16[768,768]{1,0:T(8,128)(2,1)}, u32[]{:S(2)}) copy-start(bf16[768,768]{1,0:T(8,128)(2,1)} %param.12) | copy-start | bytes 3538948
  7.2 113.0 %all-gather.2.cloned.1.call-start = ((), (), s32[]{:S(2)}) async-start(), calls=%async_computation.8 | async-start | bytes 5898240 | tf_op jit(solution)/shard_map/all_gather | solution.py:61
  12.4 16.5 %all-to-all-start = ((s32[32,2,1]{1,2,0:T(1,128)}), s32[32,2,1]{1,2,0:T(1,128)S(1)}, u32[]{:S(2)}, u32[]{:S(2)}) async-start(s32[32,2,1]{1,2,0:T(1,128)} %bitcast), calls=%async_computation | async-start | bytes 32768 | tf_op jit(solution)/shard_map/all_to_all | solution.py:91
  42.8 6.3 %copy-start.7 = (s32[128,8]{0,1:T(8,128)S(1)}, s32[128,8]{0,1:T(8,128)}, u32[]{:S(2)}) copy-start(s32[128,8]{0,1:T(8,128)} %param.18) | copy-start | bytes 12292
  42.8 64.6 %all-to-all-start.2 = ((bf16[32,4,24,768]{3,2,1,0:T(8,128)(2,1)}), bf16[32,4,24,768]{3,2,1,0:T(8,128)(2,1)}, u32[]{:S(2)}, u32[]{:S(2)}) async-start(bf16[32,4,24,768]{3,2,1,0:T(8,128)(2,1)} %broadcast_in_dim.59), calls=%async_computation.2 | async-start | bytes 9437184 | tf_op jit(solution)/shard_map/all_to_all | solution.py:50
  50.1 2.0 copy-start.3
  59.2 7.6 %copy-start.12 = (u32[128]{0:T(128)S(1)}, u32[128]{0:T(128)}, u32[]{:S(2)}) copy-start(u32[128]{0:T(128)} %constant.113) | copy-start | bytes 1540
  59.2 8.9 %copy-start.2 = (bf16[128,768]{1,0:T(8,128)(2,1)S(1)}, bf16[128,768]{1,0:T(8,128)(2,1)}, u32[]{:S(2)}) copy-start(bf16[128,768]{1,0:T(8,128)(2,1)} %param.17) | copy-start | bytes 589828
  77.5 2.8 %copy-start.5 = (bf16[2048,768]{1,0:T(8,128)(2,1)S(1)}, bf16[2048,768]{1,0:T(8,128)(2,1)}, u32[]{:S(2)}) copy-start(bf16[2048,768]{1,0:T(8,128)(2,1)} %gather_fusion.2) | copy-start | bytes 9437188
  107.4 49.7 %all-to-all-start.4 = ((bf16[128,16,768]{2,1,0:T(8,128)(2,1)}), bf16[128,16,768]{2,1,0:T(8,128)(2,1)}, u32[]{:S(2)}, u32[]{:S(2)}) async-start(bf16[128,16,768]{2,1,0:T(8,128)(2,1)} %broadcast_select_fusion), calls=%async_computation.4 | async-start | bytes 6291456 | tf_op jit(solution)/shard_map/all_to_all | solution.py:127
  115.3 4.9 %copy-start.11 = (f32[768]{0:T(1024)S(1)}, f32[768]{0:T(1024)}, u32[]{:S(2)}) copy-start(f32[768]{0:T(1024)} %param.13) | copy-start | bytes 9220
  120.2 26.7 %copy-start.8 = (f32[768]{0:T(1024)S(1)}, f32[768]{0:T(1024)}, u32[]{:S(2)}) copy-start(f32[768]{0:T(1024)} %param.14) | copy-start | bytes 9220
  151.5 28.0 %copy-start.10 = (bf16[1024,768]{1,0:T(8,128)(2,1)S(1)}, bf16[1024,768]{1,0:T(8,128)(2,1)}, u32[]{:S(2)}) copy-start(bf16[1024,768]{1,0:T(8,128)(2,1)} %param.15) | copy-start | bytes 4718596
  157.2 11.2 %all-to-all-start.3 = ((bf16[32,2,768]{2,1,0:T(2,128)(2,1)}), bf16[32,2,768]{2,1,0:T(2,128)(2,1)S(1)}, u32[]{:S(2)}, u32[]{:S(2)}) async-start(bf16[32,2,768]{2,1,0:T(2,128)(2,1)} %broadcast_select_fusion.2), calls=%async_computation.3 | async-start | bytes 196608 | tf_op jit(solution)/shard_map/all_to_all | solution.py:90
  168.4 11.7 %copy-start.4 = (bf16[128,16,768]{2,0,1:T(8,128)(2,1)S(1)}, bf16[128,16,768]{2,0,1:T(8,128)(2,1)}, u32[]{:S(2)}) copy-start(bf16[128,16,768]{2,0,1:T(8,128)(2,1)} %copy.61) | copy-start | bytes 9437188
  180.1 1.2 copy-start.6
  182.1 18.4 %all-to-all-start.5 = ((f32[128,16,1]{1,2,0:T(1,128)}), f32[128,16,1]{1,2,0:T(1,128)S(1)}, u32[]{:S(2)}, u32[]{:S(2)}) async-start(f32[128,16,1]{1,2,0:T(1,128)} %copy.62), calls=%async_computation.5 | async-start | bytes 131072 | tf_op jit(solution)/shard_map/all_to_all | solution.py:143
  200.5 14.0 %all-to-all-start.6 = ((f32[128,16,1]{1,2,0:T(1,128)}), f32[128,16,1]{1,2,0:T(1,128)S(1)}, u32[]{:S(2)}, u32[]{:S(2)}) async-start(f32[128,16,1]{1,2,0:T(1,128)} %copy.63), calls=%async_computation.6 | async-start | bytes 131072 | tf_op jit(solution)/shard_map/all_to_all | solution.py:146
  213.8 10.2 %copy-start.9 = (s32[128]{0:T(128)S(1)}, s32[128]{0:T(128)}, u32[]{:S(2)}) copy-start(s32[128]{0:T(128)} %param.19) | copy-start | bytes 1540
  214.5 51.4 %all-to-all-start.7 = ((bf16[128,16,768]{2,1,0:T(8,128)(2,1)}), bf16[128,16,768]{2,1,0:T(8,128)(2,1)}, u32[]{:S(2)}, u32[]{:S(2)}) async-start(bf16[128,16,768]{2,1,0:T(8,128)(2,1)} %copy.66), calls=%async_computation.7 | async-start | bytes 6291456 | tf_op jit(solution)/shard_map/all_to_all | solution.py:140
  265.9 8.3 %copy-start.1 = (bf16[768,768]{1,0:T(8,128)(2,1)S(1)}, bf16[768,768]{1,0:T(8,128)(2,1)}, u32[]{:S(2)}) copy-start(bf16[768,768]{1,0:T(8,128)(2,1)} %param.12) | copy-start | bytes 3538948
Sparse Core Ops, SparseCore 0:
  9.6 57.1 all-gather.1
where the time goes:
time: 282 us; the launch traced here: 281 us
  waiting for transfers between devices  67.8 us (24%)
  local copies, waits for them, and re-layouts  64.8 us (23%)
  starting transfers between devices  49.5 us (18%)
  matrix products  33.5 us (12%)
  blocking collectives  27.8 us (10%)
  other arithmetic  22.3 us (8%)
  between operations  15.2 us (5%)
    dot_general x1, matrix products, shards(): mixed = jnp.dot(hidden, w_out_full, preferred_element_type=jnp.float32)  26.7 us
    all_to_all x1, waiting for transfers between devices, shards(): lax.all_to_all(mixture.reshape(-1, width), CACHE + ('mp',), split_axis=0,...  25.9 us
    all_to_all x1, waiting for transfers between devices, shards(): lax.all_to_all(jnp.broadcast_to(mp_pieces[None], (piece_count,) + mp_piec...  17.9 us
    all_to_all x1, blocking collectives, shards(): lax.all_to_all(jnp.broadcast_to(own_piece[None], (mp_count,) + own_piece....  11.1 us
    all_gather x1, blocking collectives, shards(): lax.all_gather(got_rows, 'mp', axis=0, tiled=True)  11 us
    all_to_all x1, starting transfers between devices, shards(): lax.all_to_all(out_ids, CACHE, split_axis=0, concat_axis=0, tiled=True)  9.59 us
    all_to_all x1, starting transfers between devices, shards(): lax.all_to_all(mixture.reshape(-1, width), CACHE + ('mp',), split_axis=0,...  9.45 us
    gather x1, local copies, waits for them, and re-layouts, shards(): queries[jnp.maximum(slot_pair, 0) // neg_count]  9.41 us
  transfers between devices with their start and end apart: 8, of which 7 were waited for; matrix products, arithmetic and copies ran while one was open for 38% of the time, Pallas kernels for 0%

commit v1 on v0

--- a/solution.py
+++ b/solution.py
@@ -14,6 +14,26 @@
 def norm_rows(values):
     values = values.astype(jnp.float32)
     return values * lax.rsqrt(jnp.mean(values * values, axis=-1, keepdims=True) + epsilon)
+
+
+def bf16_part(values):
+    return lax.reduce_precision(values, exponent_bits=8, mantissa_bits=7)
+
+
+def split_parts(peak, total, width):
+    parts = []
+    for values in (peak, total):
+        high = bf16_part(values)
+        rest = values - high
+        middle = bf16_part(rest)
+        parts += [high, middle, rest - middle]
+    pad = 128 - len(parts)
+    stacked = jnp.stack(parts, axis=-1).astype(jnp.bfloat16)
+    return jnp.pad(stacked, [(0, 0)] * (stacked.ndim - 1) + [(0, pad)])
+
+
+def join_parts(parts):
+    return (parts[:, 0] + parts[:, 1]) + parts[:, 2]
 
 
 def shards(
@@ -48,13 +68,13 @@
         tiled=True,
     )
     all_pieces = lax.all_to_all(
-        jnp.broadcast_to(mp_pieces[None], (piece_count,) + mp_pieces.shape),
+        jnp.broadcast_to(mp_pieces[:, None], (mp_count, piece_count) + own_piece.shape),
         CACHE,
-        split_axis=0,
-        concat_axis=0,
+        split_axis=1,
+        concat_axis=1,
         tiled=True,
     )
-    w_out_full = jnp.transpose(all_pieces, (1, 0, 2, 3)).reshape(-1, width)
+    w_out_full = all_pieces.reshape(-1, width)
     hidden = jnp.maximum(
         jnp.dot(
             normed,
@@ -63,6 +83,7 @@
         ),
         0.0,
     ).astype(jnp.bfloat16)
+    hidden = lax.optimization_barrier(hidden)
     mixed = jnp.dot(hidden, w_out_full, preferred_element_type=jnp.float32)
     state_sum = tokens.astype(jnp.float32) + mixed
     final_rows = norm_rows(state_sum) * gain_out
@@ -136,20 +157,16 @@
     block_total = jnp.sum(exp_terms, axis=-1)
     weights = exp_terms.astype(jnp.bfloat16)
     mixture = jnp.einsum("snkr,nrd->snkd", weights, block_keys, preferred_element_type=jnp.float32)
-    back_mix, back_peak, back_total = (
-        lax.all_to_all(
-            mixture.reshape(-1, width), CACHE + ("mp",), split_axis=0, concat_axis=0, tiled=True
-        ),
-        lax.all_to_all(
-            block_peak.reshape(-1), CACHE + ("mp",), split_axis=0, concat_axis=0, tiled=True
-        ),
-        lax.all_to_all(
-            block_total.reshape(-1), CACHE + ("mp",), split_axis=0, concat_axis=0, tiled=True
-        ),
-    )
-    pair_mix = back_mix[pair_slots].reshape(query_count, neg_count, width)
-    pair_peak = back_peak[pair_slots].reshape(query_count, neg_count)
-    pair_total = back_total[pair_slots].reshape(query_count, neg_count)
+    packed = jnp.concatenate(
+        [mixture.astype(jnp.bfloat16), split_parts(block_peak, block_total, width)], axis=-1
+    )
+    back = lax.all_to_all(
+        packed.reshape(-1, packed.shape[-1]), CACHE + ("mp",), split_axis=0, concat_axis=0, tiled=True
+    )
+    pair_back = back[pair_slots].astype(jnp.float32)
+    pair_mix = pair_back[:, :width].reshape(query_count, neg_count, width)
+    pair_peak = join_parts(pair_back[:, width : width + 3]).reshape(query_count, neg_count)
+    pair_total = join_parts(pair_back[:, width + 3 : width + 6]).reshape(query_count, neg_count)
     pick_table = (positive_ids[:, None] == jnp.arange(docs_here, dtype=jnp.int32)[None, :]).astype(
         jnp.bfloat16
     )

time: 282 us -> 266 us (0.943)
  starting transfers between devices: 49.5 us -> 36.3 us
  local copies, waits for them, and re-layouts: 64.8 us -> 52.1 us
  waiting for transfers between devices: 67.8 us -> 80 us
    dot_general x0 -> x1, matrix products: none -> 15.8 us  [shards(): jnp.dot(normed, lax.all_gather(w_in, 'mp', axis=1, tiled=True), preferred...]
    dot_general x1, matrix products: 26.7 us -> 13.4 us  [shards(): mixed = jnp.dot(hidden, w_out_full, preferred_element_type=jnp.float32)]
    all_to_all x4 -> x2, starting transfers between devices: 28.3 us -> 15.1 us  [the longest x1 8.89 us: shards(): lax.all_to_all(packed.reshape(-1, packed.shape[-1]), CACHE + ('mp',), spl...]
    gather x3 -> x1, local copies, waits for them, and re-layouts: 19.2 us -> 7.17 us  [shards(): pair_back = back[pair_slots].astype(jnp.float32)]
    all_to_all x4 -> x2, waiting for transfers between devices: 53.5 us -> 65 us  [the longest x1 47.2 us: shards(): lax.all_to_all(packed.reshape(-1, packed.shape[-1]), CACHE + ('mp',), spl...]
    dot_general x1, matrix products: 4.14 us -> 1.03 us  [shards(): jnp.einsum('snkr,nrd->snkd', weights, block_keys, preferred_element_type=...]
    reduce_sum x1, other arithmetic: 4.38 us -> 1.37 us  [shards(): pooled = jnp.mean(final_rows.reshape(docs_here, doc_len, width), axis=1)]
    all_to_all x7 -> x2, local copies, waits for them, and re-layouts: 12 us -> 11.3 us  [the longest x1 6.52 us: shards(): lax.all_to_all(packed.reshape(-1, packed.shape[-1]), CACHE + ('mp',), spl...]
  transfers between devices with their start and end apart: 8 -> 6, of which waited for: 7 -> 5; matrix products, arithmetic and copies ran while one was open for 38% -> 30% of each run, Pallas kernels for 0% -> 0%
where the time goes in v1:
time: 266 us; the launch traced here: 265 us
  waiting for transfers between devices  80 us (30%)
  local copies, waits for them, and re-layouts  52.1 us (20%)
  starting transfers between devices  36.3 us (14%)
  matrix products  33 us (12%)
  blocking collectives  27.4 us (10%)
  other arithmetic  21.4 us (8%)
  between operations  15.2 us (6%)
    all_to_all x1, waiting for transfers between devices, shards(): lax.all_to_all(packed.reshape(-1, packed.shape[-1]), CACHE + ('mp',), spl...  47.2 us
    all_to_all x1, waiting for transfers between devices, shards(): lax.all_to_all(jnp.broadcast_to(mp_pieces[:, None], (mp_count, piece_coun...  17.8 us
    dot_general x1, matrix products, shards(): jnp.dot(normed, lax.all_gather(w_in, 'mp', axis=1, tiled=True), preferred...  15.8 us
    dot_general x1, matrix products, shards(): mixed = jnp.dot(hidden, w_out_full, preferred_element_type=jnp.float32)  13.4 us
    all_to_all x1, blocking collectives, shards(): lax.all_to_all(jnp.broadcast_to(own_piece[None], (mp_count,) + own_piece....  11.1 us
    all_gather x1, blocking collectives, shards(): lax.all_gather(got_rows, 'mp', axis=0, tiled=True)  10.6 us
    all_to_all x1, starting transfers between devices, shards(): lax.all_to_all(out_ids, CACHE, split_axis=0, concat_axis=0, tiled=True)  9.59 us
    gather x1, local copies, waits for them, and re-layouts, shards(): queries[jnp.maximum(slot_pair, 0) // neg_count]  9.44 us
  transfers between devices with their start and end apart: 6, of which 5 were waited for; matrix products, arithmetic and copies ran while one was open for 30% of the time, Pallas kernels for 0%

profile of v1, /device:TPU:1, one launch (start us, length us, event | category | flops | bytes accessed | tf_op | source)
XLA Modules:
  0.0 265.2 jit_solution(6953514105947206072)
XLA Ops:
  12.4 9.6 %all-to-all-start = ((s32[32,2,1]{1,2,0:T(1,128)}), s32[32,2,1]{1,2,0:T(1,128)S(1)}, u32[]{:S(2)}, u32[]{:S(2)}) async-start(s32[32,2,1]{1,2,0:T(1,128)} %bitcast), calls=%async_computation | async-start | bytes 32768 | tf_op jit(solution)/shard_map/all_to_all | solution.py:112
  22.1 6.9 %all-to-all-done = s32[32,2,1]{1,2,0:T(1,128)S(1)} async-done(((s32[32,2,1]{1,2,0:T(1,128)}), s32[32,2,1]{1,2,0:T(1,128)S(1)}, u32[]{:S(2)}, u32[]{:S(2)}) %all-to-all-start) | async-done | bytes 288 | tf_op jit(solution)/shard_map/all_to_all | solution.py:112
  28.9 11.1 %all_to_all.49 = bf16[4,24,768]{2,1,0:T(8,128)(2,1)S(1)} all-to-all(bf16[4,24,768]{2,1,0:T(8,128)(2,1)S(1)} %broadcast_in_dim.58), channel_id=1, replica_groups=mesh['chip'=16,'core'=2,'mp'=4] {'mp'}, dimensions={0} | all-to-all | bytes 294912 | tf_op jit(solution)/shard_map/all_to_all | solution.py:63
  42.8 6.2 %all-to-all-start.2 = ((bf16[4,32,24,768]{3,2,0,1:T(8,128)(2,1)}), bf16[4,32,24,768]{3,2,0,1:T(8,128)(2,1)}, u32[]{:S(2)}, u32[]{:S(2)}) async-start(bf16[4,32,24,768]{3,2,0,1:T(8,128)(2,1)} %broadcast_in_dim.94), calls=%async_computation.2 | async-start | bytes 9437184 | tf_op jit(solution)/shard_map/all_to_all | solution.py:70
  54.8 4.4 %copy.78 = s32[1024,8,128]{0,2,1:T(8,128)} copy(s32[1024,8,128]{0,1,2:T(8,128)S(1)} %add_add_fusion) | data formatting | bytes 8388608 | tf_op jit(solution)/shard_map/sub | solution.py:136
  59.4 2.9 %fusion.4 = s32[1024]{0:T(1024)S(1)} fusion(s32[1024,8,128]{0,2,1:T(8,128)} %copy.78, s32[1024]{0:T(1024)S(1)} %eq.70), kind=kLoop, calls=%fused_computation.19 | loop fusion | flops 3144704 | bytes 4202496 | tf_op jit(solution)/shard_map/reduce_sum | solution.py:136
  62.4 4.3 %scatter_custom_fusion.1 = s32[2048]{0:T(1024)S(1)} fusion(s32[1024]{0:T(1024)S(1)} %bitcast.88, s32[1024]{0:T(1024)S(1)} %iota.25, s32[]{:T(128)} %constant.37.clone.1), kind=kCustom, calls=%fused_computation.95 | custom fusion | bytes 8196 | tf_op jit(solution)/shard_map/scatter | solution.py:141
  68.1 9.4 %gather_fusion.2 = bf16[2048,768]{1,0:T(8,128)(2,1)} fusion(bf16[128,768]{1,0:T(8,128)(2,1)S(1)} %copy-done.2, s32[2048]{0:T(1024)S(1)} %fusion.30), kind=kCustom, calls=%fused_computation.2 | custom fusion | bytes 6299648 | tf_op jit(solution)/shard_map/gather | solution.py:145
  77.5 2.7 %fusion.1 = f32[2048]{0:T(1024)S(1)} fusion(bf16[2048,768]{1,0:T(8,128)(2,1)} %param.10), kind=kLoop, calls=%fused_computation.12 | loop fusion | flops 4716544 | bytes 3153920 | tf_op jit(solution)/shard_map/reduce_sum | solution.py:16
  83.9 5.7 %all-reduce.1 = s32[256]{0:T(256)S(1)} all-reduce(s32[256]{0:T(256)S(1)} %dynamic-update-slice), channel_id=1, replica_groups=mesh['chip'=16,'core'=2,'mp'=4] {'mp'}, use_global_device_ids=true, to_apply=%add.1 | all-reduce | flops 256 | bytes 2048
  89.6 17.8 %all-to-all-done.2 = bf16[4,32,24,768]{3,2,0,1:T(8,128)(2,1)} async-done(((bf16[4,32,24,768]{3,2,0,1:T(8,128)(2,1)}), bf16[4,32,24,768]{3,2,0,1:T(8,128)(2,1)}, u32[]{:S(2)}, u32[]{:S(2)}) %all-to-all-start.2) | async-done | bytes 4718624 | tf_op jit(solution)/shard_map/all_to_all | solution.py:70
  107.4 7.8 %all-to-all-start.4 = ((bf16[128,16,768]{2,1,0:T(8,128)(2,1)}), bf16[128,16,768]{2,1,0:T(8,128)(2,1)}, u32[]{:S(2)}, u32[]{:S(2)}) async-start(bf16[128,16,768]{2,1,0:T(8,128)(2,1)} %broadcast_select_fusion), calls=%async_computation.4 | async-start | bytes 6291456 | tf_op jit(solution)/shard_map/all_to_all | solution.py:148
  115.3 4.8 %copy.73 = bf16[4,32,24,768]{3,2,1,0:T(8,128)(2,1)} copy(bf16[4,32,24,768]{3,2,0,1:T(8,128)(2,1)} %all-to-all-done.2) | data formatting | bytes 9437184 | tf_op jit(solution)/shard_map/all_to_all | solution.py:70
  120.1 15.8 %maximum_convert_fusion = bf16[2048,3072]{1,0:T(8,128)(2,1)} fusion(bf16[768,3072]{1,0:T(8,128)(2,1)} %all-gather.2.cloned.1.call-done, bf16[2048,768]{1,0:T(8,128)(2,1)} %param.10, f32[768]{0:T(1024)S(1)} %copy-done.13, f32[2048]{0:T(1024)S(1)} %add_rsqrt_fusion.1), kind=kOutput, calls=%fused_computation.6 | convolution fusion | flops 9682550784 | bytes 20458496 | tf_op jit(solution)/shard_map/dot_general | solution.py:79
  135.9 13.4 %multiply_reduce_fusion = (f32[2048]{0:T(1024)S(1)}, f32[2048,768]{1,0:T(8,128)S(1)}) fusion(bf16[2048,768]{1,0:T(8,128)(2,1)S(1)} %copy-done.4, bf16[2048,3072]{1,0:T(8,128)(2,1)} %maximum_convert_fusion, bf16[3072,768]{1,0:T(8,128)(2,1)S(1)} %bitcast.86), kind=kOutput, calls=%fused_computation.17 | convolution fusion | flops 9669965824 | bytes 26746880 | tf_op jit(solution)/shard_map/dot_general | solution.py:87
  152.5 4.6 %all-to-all-done.4 = bf16[128,16,768]{2,1,0:T(8,128)(2,1)} async-done(((bf16[128,16,768]{2,1,0:T(8,128)(2,1)}), bf16[128,16,768]{2,1,0:T(8,128)(2,1)}, u32[]{:S(2)}, u32[]{:S(2)}) %all-to-all-start.4) | async-done | bytes 3145760 | tf_op jit(solution)/shard_map/all_to_all | solution.py:148
  157.1 3.7 %all-to-all-start.3 = ((bf16[32,2,768]{2,1,0:T(2,128)(2,1)}), bf16[32,2,768]{2,1,0:T(2,128)(2,1)S(1)}, u32[]{:S(2)}, u32[]{:S(2)}) async-start(bf16[32,2,768]{2,1,0:T(2,128)(2,1)} %broadcast_select_fusion.2), calls=%async_computation.3 | async-start | bytes 196608 | tf_op jit(solution)/shard_map/all_to_all | solution.py:111
  161.0 4.6 %copy.79 = bf16[128,16,768]{2,0,1:T(8,128)(2,1)} copy(bf16[128,16,768]{2,1,0:T(8,128)(2,1)} %all-to-all-done.4) | data formatting | bytes 6291456 | tf_op jit(solution)/shard_map/all_to_all | solution.py:148
  165.6 2.8 %all-to-all-done.3 = bf16[32,2,768]{2,1,0:T(2,128)(2,1)S(1)} async-done(((bf16[32,2,768]{2,1,0:T(2,128)(2,1)}), bf16[32,2,768]{2,1,0:T(2,128)(2,1)S(1)}, u32[]{:S(2)}, u32[]{:S(2)}) %all-to-all-start.3) | async-done | bytes 98336 | tf_op jit(solution)/shard_map/all_to_all | solution.py:111
  168.4 10.6 %all_gather.11 = bf16[256,768]{1,0:T(8,128)(2,1)S(1)} all-gather(bf16[64,768]{1,0:T(8,128)(2,1)S(1)} %all_to_all.38), channel_id=1, replica_groups=mesh['chip'=16,'core'=2,'mp'=4] {'mp'}, dimensions={0}, use_global_device_ids=true | all-gather | bytes 491520 | tf_op jit(solution)/shard_map/all_gather | solution.py:115
  184.5 6.5 %copy.85 = bf16[128,16,896]{2,1,0:T(8,128)(2,1)} copy(bf16[128,16,896]{0,2,1:T(8,128)(2,1)} %bitcast.81) | data formatting | bytes 7340032 | tf_op jit(solution)/shard_map/all_to_all | solution.py:163
  191.0 8.9 %all-to-all-start.5 = ((bf16[128,16,896]{2,1,0:T(8,128)(2,1)}), bf16[128,16,896]{2,1,0:T(8,128)(2,1)}, u32[]{:S(2)}, u32[]{:S(2)}) async-start(bf16[128,16,896]{2,1,0:T(8,128)(2,1)} %copy.85), calls=%async_computation.5 | async-start | bytes 7340032 | tf_op jit(solution)/shard_map/all_to_all | solution.py:163
  200.2 47.2 %all-to-all-done.5 = bf16[128,16,896]{2,1,0:T(8,128)(2,1)} async-done(((bf16[128,16,896]{2,1,0:T(8,128)(2,1)}), bf16[128,16,896]{2,1,0:T(8,128)(2,1)}, u32[]{:S(2)}, u32[]{:S(2)}) %all-to-all-start.5) | async-done | bytes 3670048 | tf_op jit(solution)/shard_map/all_to_all | solution.py:163
  247.4 7.2 %gather_fusion.3 = bf16[1024,896]{1,0:T(8,128)(2,1)S(1)} fusion(bf16[2048,896]{1,0:T(8,128)(2,1)} %bitcast.20, s32[1024]{0:T(1024)S(1)} %broadcast_clamp_fusion), kind=kCustom, calls=%fused_computation.3 | custom fusion | bytes 3674112 | tf_op jit(solution)/shard_map/gather | solution.py:166
  (110 shorter events, 31.1 us)
Async XLA Ops:
  7.2 14.9 %copy-start = (bf16[768,768]{1,0:T(8,128)(2,1)S(1)}, bf16[768,768]{1,0:T(8,128)(2,1)}, u32[]{:S(2)}) copy-start(bf16[768,768]{1,0:T(8,128)(2,1)} %param.12) | copy-start | bytes 3538948
  7.2 112.9 %all-gather.2.cloned.1.call-start = ((), (), s32[]{:S(2)}) async-start(), calls=%async_computation.6 | async-start | bytes 5898240 | tf_op jit(solution)/shard_map/all_gather | solution.py:81
  12.4 16.5 %all-to-all-start = ((s32[32,2,1]{1,2,0:T(1,128)}), s32[32,2,1]{1,2,0:T(1,128)S(1)}, u32[]{:S(2)}, u32[]{:S(2)}) async-start(s32[32,2,1]{1,2,0:T(1,128)} %bitcast), calls=%async_computation | async-start | bytes 32768 | tf_op jit(solution)/shard_map/all_to_all | solution.py:112
  42.8 6.3 %copy-start.9 = (s32[128,8]{0,1:T(8,128)S(1)}, s32[128,8]{0,1:T(8,128)}, u32[]{:S(2)}) copy-start(s32[128,8]{0,1:T(8,128)} %param.18) | copy-start | bytes 12292
  42.8 64.7 %all-to-all-start.2 = ((bf16[4,32,24,768]{3,2,0,1:T(8,128)(2,1)}), bf16[4,32,24,768]{3,2,0,1:T(8,128)(2,1)}, u32[]{:S(2)}, u32[]{:S(2)}) async-start(bf16[4,32,24,768]{3,2,0,1:T(8,128)(2,1)} %broadcast_in_dim.94), calls=%async_computation.2 | async-start | bytes 9437184 | tf_op jit(solution)/shard_map/all_to_all | solution.py:70
  50.0 2.0 copy-start.3
  59.2 7.6 %copy-start.14 = (u32[128]{0:T(128)S(1)}, u32[128]{0:T(128)}, u32[]{:S(2)}) copy-start(u32[128]{0:T(128)} %constant.116) | copy-start | bytes 1540
  59.2 8.9 %copy-start.2 = (bf16[128,768]{1,0:T(8,128)(2,1)S(1)}, bf16[128,768]{1,0:T(8,128)(2,1)}, u32[]{:S(2)}) copy-start(bf16[128,768]{1,0:T(8,128)(2,1)} %param.17) | copy-start | bytes 589828
  77.5 2.8 %copy-start.6 = (bf16[2048,768]{1,0:T(8,128)(2,1)S(1)}, bf16[2048,768]{1,0:T(8,128)(2,1)}, u32[]{:S(2)}) copy-start(bf16[2048,768]{1,0:T(8,128)(2,1)} %gather_fusion.2) | copy-start | bytes 9437188
  107.4 49.7 %all-to-all-start.4 = ((bf16[128,16,768]{2,1,0:T(8,128)(2,1)}), bf16[128,16,768]{2,1,0:T(8,128)(2,1)}, u32[]{:S(2)}, u32[]{:S(2)}) async-start(bf16[128,16,768]{2,1,0:T(8,128)(2,1)} %broadcast_select_fusion), calls=%async_computation.4 | async-start | bytes 6291456 | tf_op jit(solution)/shard_map/all_to_all | solution.py:148
  115.3 4.8 %copy-start.13 = (f32[768]{0:T(1024)S(1)}, f32[768]{0:T(1024)}, u32[]{:S(2)}) copy-start(f32[768]{0:T(1024)} %param.13) | copy-start | bytes 9220
  120.1 15.8 %copy-start.4 = (bf16[2048,768]{1,0:T(8,128)(2,1)S(1)}, bf16[2048,768]{1,0:T(8,128)(2,1)}, u32[]{:S(2)}) copy-start(bf16[2048,768]{1,0:T(8,128)(2,1)} %param.10) | copy-start | bytes 9437188
  120.1 15.8 %copy-start.8 = (bf16[4,32,24,768]{3,2,1,0:T(8,128)(2,1)S(1)}, bf16[4,32,24,768]{3,2,1,0:T(8,128)(2,1)}, u32[]{:S(2)}) copy-start(bf16[4,32,24,768]{3,2,1,0:T(8,128)(2,1)} %copy.73) | copy-start | bytes 14155780
  135.9 13.4 %copy-start.10 = (f32[768]{0:T(1024)S(1)}, f32[768]{0:T(1024)}, u32[]{:S(2)}) copy-start(f32[768]{0:T(1024)} %param.14) | copy-start | bytes 9220
  150.9 28.1 %copy-start.12 = (bf16[1024,768]{1,0:T(8,128)(2,1)S(1)}, bf16[1024,768]{1,0:T(8,128)(2,1)}, u32[]{:S(2)}) copy-start(bf16[1024,768]{1,0:T(8,128)(2,1)} %param.15) | copy-start | bytes 4718596
  157.1 11.2 %all-to-all-start.3 = ((bf16[32,2,768]{2,1,0:T(2,128)(2,1)}), bf16[32,2,768]{2,1,0:T(2,128)(2,1)S(1)}, u32[]{:S(2)}, u32[]{:S(2)}) async-start(bf16[32,2,768]{2,1,0:T(2,128)(2,1)} %broadcast_select_fusion.2), calls=%async_computation.3 | async-start | bytes 196608 | tf_op jit(solution)/shard_map/all_to_all | solution.py:111
  168.4 11.3 %copy-start.5 = (bf16[128,16,768]{2,0,1:T(8,128)(2,1)S(1)}, bf16[128,16,768]{2,0,1:T(8,128)(2,1)}, u32[]{:S(2)}) copy-start(bf16[128,16,768]{2,0,1:T(8,128)(2,1)} %copy.79) | copy-start | bytes 9437188
  179.7 2.2 copy-start.7
  191.0 8.9 %copy-start.11 = (s32[128]{0:T(128)S(1)}, s32[128]{0:T(128)}, u32[]{:S(2)}) copy-start(s32[128]{0:T(128)} %param.19) | copy-start | bytes 1540
  191.0 56.4 %all-to-all-start.5 = ((bf16[128,16,896]{2,1,0:T(8,128)(2,1)}), bf16[128,16,896]{2,1,0:T(8,128)(2,1)}, u32[]{:S(2)}, u32[]{:S(2)}) async-start(bf16[128,16,896]{2,1,0:T(8,128)(2,1)} %copy.85), calls=%async_computation.5 | async-start | bytes 7340032 | tf_op jit(solution)/shard_map/all_to_all | solution.py:163
  254.6 3.8 %copy-start.1 = (bf16[768,768]{1,0:T(8,128)(2,1)S(1)}, bf16[768,768]{1,0:T(8,128)(2,1)}, u32[]{:S(2)}) copy-start(bf16[768,768]{1,0:T(8,128)(2,1)} %param.12) | copy-start | bytes 3538948
Sparse Core Ops, SparseCore 0:
  9.7 57.1 all-gather.1

commit v2 on v1

--- a/solution.py
+++ b/solution.py
@@ -9,6 +9,7 @@
 
 epsilon = 1e-06
 CACHE = ("chip", "core")
+CODE_BASE = 32
 
 
 def norm_rows(values):
@@ -59,6 +60,7 @@
     piece_count = cache_count
     piece_rows = w_out.shape[0] // piece_count
     piece_at = lax.axis_index(CACHE) * piece_rows
+    mp_here = lax.axis_index("mp")
     own_piece = lax.dynamic_slice_in_dim(w_out, piece_at, piece_rows, axis=0)
     mp_pieces = lax.all_to_all(
         jnp.broadcast_to(own_piece[None], (mp_count,) + own_piece.shape),
@@ -67,64 +69,74 @@
         concat_axis=0,
         tiled=True,
     )
-    all_pieces = lax.all_to_all(
-        jnp.broadcast_to(mp_pieces[:, None], (mp_count, piece_count) + own_piece.shape),
+    mp_twice = jnp.concatenate([mp_pieces, mp_pieces], axis=0)
+    other_pieces = lax.dynamic_slice_in_dim(mp_twice, mp_here + 1, mp_count - 1, axis=0)
+    rest_pieces = lax.all_to_all(
+        jnp.broadcast_to(other_pieces[:, None], (mp_count - 1, piece_count) + own_piece.shape),
         CACHE,
         split_axis=1,
         concat_axis=1,
         tiled=True,
     )
-    w_out_full = all_pieces.reshape(-1, width)
-    hidden = jnp.maximum(
-        jnp.dot(
-            normed,
-            lax.all_gather(w_in, "mp", axis=1, tiled=True),
-            preferred_element_type=jnp.float32,
-        ),
-        0.0,
+    w_out_rest = rest_pieces.reshape(-1, width)
+    w_in_full = lax.all_gather(w_in, "mp", axis=1, tiled=True)
+    shard_cols = w_in.shape[1]
+    w_in_rest = lax.dynamic_slice_in_dim(
+        jnp.concatenate([w_in_full, w_in_full], axis=1),
+        (mp_here + 1) * shard_cols,
+        (mp_count - 1) * shard_cols,
+        axis=1,
+    )
+    hidden_own = jnp.maximum(
+        jnp.dot(normed, w_in, preferred_element_type=jnp.float32), 0.0
     ).astype(jnp.bfloat16)
-    hidden = lax.optimization_barrier(hidden)
-    mixed = jnp.dot(hidden, w_out_full, preferred_element_type=jnp.float32)
+    hidden_rest = jnp.maximum(
+        jnp.dot(normed, w_in_rest, preferred_element_type=jnp.float32), 0.0
+    ).astype(jnp.bfloat16)
+    mixed = jnp.dot(hidden_own, w_out, preferred_element_type=jnp.float32) + jnp.dot(
+        hidden_rest, w_out_rest, preferred_element_type=jnp.float32
+    )
     state_sum = tokens.astype(jnp.float32) + mixed
     final_rows = norm_rows(state_sum) * gain_out
     pooled = jnp.mean(final_rows.reshape(docs_here, doc_len, width), axis=1)
     embedded = norm_rows(pooled).astype(jnp.bfloat16)
     rows_own = stale_cache.shape[0]
-    group_rows = rows_own * mp_count
+    device_count = cache_count * mp_count
     refresh_cap = 2 * docs_here // cache_count
-    group_of = refresh_ids // group_rows
-    group_hits = (group_of[:, None] == jnp.arange(cache_count, dtype=jnp.int32)[None, :]).astype(
+    dest_of = refresh_ids // rows_own
+    dest_hits = (dest_of[:, None] == jnp.arange(device_count, dtype=jnp.int32)[None, :]).astype(
         jnp.int32
     )
-    rank_in = jnp.sum(group_hits * (jnp.cumsum(group_hits, axis=0) - 1), axis=1)
-    slot_of = group_of * refresh_cap + rank_in
+    rank_in = jnp.sum(dest_hits * (jnp.cumsum(dest_hits, axis=0) - 1), axis=1)
+    slot_of = dest_of * refresh_cap + rank_in
     filled = (
-        jnp.full((cache_count * refresh_cap,), -1, jnp.int32)
+        jnp.full((device_count * refresh_cap,), -1, jnp.int32)
         .at[slot_of]
         .set(jnp.arange(docs_here, dtype=jnp.int32))
     )
     slot_used = filled >= 0
     slot_doc = jnp.maximum(filled, 0)
-    out_rows = jnp.where(slot_used[:, None], embedded[slot_doc], jnp.zeros((), jnp.bfloat16))
-    out_ids = jnp.where(slot_used, refresh_ids[slot_doc], -1)
-    got_rows, got_ids = (
-        lax.all_to_all(out_rows, CACHE, split_axis=0, concat_axis=0, tiled=True),
-        lax.all_to_all(out_ids, CACHE, split_axis=0, concat_axis=0, tiled=True),
-    )
-    all_rows, all_ids = (
-        lax.all_gather(got_rows, "mp", axis=0, tiled=True),
-        lax.all_gather(got_ids, "mp", axis=0, tiled=True),
-    )
-    row_base = (lax.axis_index(CACHE) * mp_count + lax.axis_index("mp")) * rows_own
-    local_row = all_ids - row_base
+    code = jnp.where(slot_used, refresh_ids[slot_doc] % rows_own + 1, 0)
+    code_cols = jnp.zeros((code.shape[0], 128), jnp.float32)
+    code_cols = code_cols.at[:, 0].set((code // CODE_BASE).astype(jnp.float32))
+    code_cols = code_cols.at[:, 1].set((code % CODE_BASE).astype(jnp.float32))
+    out_rows = jnp.concatenate(
+        [
+            jnp.where(slot_used[:, None], embedded[slot_doc], jnp.zeros((), jnp.bfloat16)),
+            code_cols.astype(jnp.bfloat16),
+        ],
+        axis=1,
+    )
+    got = lax.all_to_all(out_rows, CACHE + ("mp",), split_axis=0, concat_axis=0, tiled=True)
+    got_code = got[:, width].astype(jnp.int32) * CODE_BASE + got[:, width + 1].astype(jnp.int32)
+    local_row = got_code - 1
     write_table = jnp.arange(rows_own, dtype=jnp.int32)[:, None] == local_row[None, :]
     placed = jnp.dot(
-        write_table.astype(jnp.bfloat16), all_rows, preferred_element_type=jnp.float32
+        write_table.astype(jnp.bfloat16), got[:, :width], preferred_element_type=jnp.float32
     ).astype(jnp.bfloat16)
     written = jnp.any(write_table, axis=1)
     fresh_cache = jnp.where(written[:, None], placed, stale_cache)
     local_blocks = rows_own // BLOCK
-    device_count = cache_count * mp_count
     block_count = local_blocks * device_count
     query_count, neg_count = neg_blocks.shape
     pair_count = query_count * neg_count

time: 266 us -> 264 us (level)
  blocking collectives: 27.4 us -> 0 us
  other arithmetic: 21.4 us -> 46.9 us
  starting transfers between devices: 36.3 us -> 31.9 us
  matrix products: 33 us -> 36.3 us
    another operation x3 -> x7, other arithmetic: 0.57 us -> 23.2 us
    all_to_all x1 -> x0, blocking collectives: 11.1 us -> none  [shards(): lax.all_to_all(jnp.broadcast_to(own_piece[None], (mp_count,) + own_piece....]
    all_gather x1 -> x0, blocking collectives: 10.6 us -> none  [shards(): lax.all_gather(got_rows, 'mp', axis=0, tiled=True)]
    unnamed x1 -> x0, blocking collectives: 5.68 us -> none
    all_to_all x3, waiting for transfers between devices: 27.5 us -> 22 us  [the longest x1 13.2 us: shards(): lax.all_to_all(jnp.broadcast_to(other_pieces[:, None], (mp_count - 1, pie...]
    all_to_all x1, waiting for transfers between devices: 4.63 us -> 9.21 us  [shards(): lax.all_to_all(outbound, CACHE + ('mp',), split_axis=0, concat_axis=0, ti...]
    all_to_all x1, starting transfers between devices: 8.89 us -> 4.82 us  [shards(): lax.all_to_all(packed.reshape(-1, packed.shape[-1]), CACHE + ('mp',), spl...]
    dot_general x3, matrix products: 29.9 us -> 33.2 us  [the longest x1 22.3 us: shards(): jnp.dot(hidden_rest, w_out_rest, preferred_element_type=jnp.float32)]
  transfers between devices with their start and end apart: 6 -> 6, of which waited for: 5 -> 4; matrix products, arithmetic and copies ran while one was open for 30% -> 41% of each run, Pallas kernels for 0% -> 0%
where the time goes in v2:
time: 264 us; the launch traced here: 263 us
  waiting for transfers between devices  79.1 us (30%)
  local copies, waits for them, and re-layouts  54.5 us (21%)
  other arithmetic  46.9 us (18%)
  matrix products  36.3 us (14%)
  starting transfers between devices  31.9 us (12%)
  between operations  14.5 us (5%)
    all_to_all x1, waiting for transfers between devices, shards(): lax.all_to_all(packed.reshape(-1, packed.shape[-1]), CACHE + ('mp',), spl...  47.2 us
    another operation x6, other arithmetic  23.1 us
    dot_general x1, matrix products, shards(): jnp.dot(hidden_rest, w_out_rest, preferred_element_type=jnp.float32)  22.3 us
    all_to_all x1, waiting for transfers between devices, shards(): lax.all_to_all(jnp.broadcast_to(other_pieces[:, None], (mp_count - 1, pie...  13.2 us
    gather x1, local copies, waits for them, and re-layouts, shards(): queries[jnp.maximum(slot_pair, 0) // neg_count]  9.38 us
    all_to_all x1, starting transfers between devices, shards(): lax.all_to_all(jnp.broadcast_to(other_pieces[:, None], (mp_count - 1, pie...  9.3 us
    all_to_all x1, waiting for transfers between devices, shards(): lax.all_to_all(outbound, CACHE + ('mp',), split_axis=0, concat_axis=0, ti...  9.21 us
    all_to_all x1, starting transfers between devices, shards(): lax.all_to_all(outbound, CACHE + ('mp',), split_axis=0, concat_axis=0, ti...  9.1 us
  transfers between devices with their start and end apart: 6, of which 4 were waited for; matrix products, arithmetic and copies ran while one was open for 41% of the time, Pallas kernels for 0%

profile of v2, /device:TPU:1, one launch (start us, length us, event | category | flops | bytes accessed | tf_op | source)
XLA Modules:
  0.0 263.2 jit_solution(14783255058550592332)
XLA Ops:
  9.1 4.8 %all-to-all-start = ((bf16[4,24,768]{2,1,0:T(8,128)(2,1)}), bf16[4,24,768]{2,1,0:T(8,128)(2,1)S(1)}, u32[]{:S(2)}, u32[]{:S(2)}) async-start(bf16[4,24,768]{2,1,0:T(8,128)(2,1)} %broadcast_in_dim.55), calls=%async_computation | async-start | bytes 294912 | tf_op jit(solution)/shard_map/all_to_all | solution.py:65
  21.8 20.7 %fusion.53 = (f32[256]{0:T(256)S(1)}, s32[256]{0:T(256)S(1)}, pred[256]{0:T(512)(128)(4,1)S(1)}) fusion(pred[]{:T(512)} %compare_reduce_fusion, s32[]{:T(128)} %bitcast.33, s32[]{:T(128)} %bitcast.32, s32[]{:T(128)} %bitcast.31, s32[]{:T(128)} %bitcast.30, s32[]{:T(128)} %bitcast.29, s32[]{:T(128)} %bitcast.28, s32[]{:T(128)} %bitcast.27, s32[]{:T(128)} %bitcast.26, ...), kind=kLoop, calls=%fused_computation.160 | loop fusion | flops 23040 | bytes 3457 | tf_op jit(solution)/shard_map/select.23
  42.5 5.2 %add_add_fusion = s32[1024,8,128]{0,1,2:T(8,128)} fusion(s32[1024,8,128]{0,1,2:T(8,128)} %copy-done.3, s32[1024,8]{0,1:T(8,128)S(1)} %slice.128), kind=kLoop, calls=%fused_computation.23 | loop fusion | flops 2097152 | bytes 8421376 | tf_op jit(solution)/shard_map/sub | solution.py:148
  48.7 6.6 %copy.102 = s32[1024,8,128]{0,2,1:T(8,128)} copy(s32[1024,8,128]{0,1,2:T(8,128)} %add_add_fusion) | data formatting | bytes 8388608 | tf_op jit(solution)/shard_map/sub | solution.py:148
  57.4 9.3 %all-to-all-start.1 = ((bf16[3,32,24,768]{3,2,0,1:T(8,128)(2,1)}), bf16[3,32,24,768]{3,2,0,1:T(8,128)(2,1)}, u32[]{:S(2)}, u32[]{:S(2)}) async-start(bf16[3,32,24,768]{3,2,0,1:T(8,128)(2,1)} %broadcast_in_dim.56), calls=%async_computation.1 | async-start | bytes 7077888 | tf_op jit(solution)/shard_map/all_to_all | solution.py:74
  66.9 2.9 %fusion.5 = s32[1024]{0:T(1024)S(1)} fusion(s32[1024,8,128]{0,2,1:T(8,128)} %copy.102, s32[1024]{0:T(1024)S(1)} %eq.73), kind=kLoop, calls=%fused_computation.22 | loop fusion | flops 3144704 | bytes 4202496 | tf_op jit(solution)/shard_map/reduce_sum | solution.py:148
  69.9 4.3 %scatter_custom_fusion.1 = s32[2048]{0:T(1024)S(1)} fusion(s32[1024]{0:T(1024)S(1)} %bitcast.119, s32[1024]{0:T(1024)S(1)} %iota.37, s32[]{:T(128)} %constant.168.clone.1), kind=kCustom, calls=%fused_computation.105 | custom fusion | bytes 8196 | tf_op jit(solution)/shard_map/scatter | solution.py:153
  74.6 9.4 %gather_fusion.1 = bf16[2048,768]{1,0:T(8,128)(2,1)} fusion(bf16[128,768]{1,0:T(8,128)(2,1)S(1)} %copy-done.2, s32[2048]{0:T(1024)S(1)} %fusion.44), kind=kCustom, calls=%fused_computation.1 | custom fusion | bytes 6299648 | tf_op jit(solution)/shard_map/gather | solution.py:157
  84.0 2.7 %fusion.1 = f32[2048]{0:T(1024)S(1)} fusion(bf16[2048,768]{1,0:T(8,128)(2,1)} %param.14), kind=kLoop, calls=%fused_computation.13 | loop fusion | flops 4716544 | bytes 3153920 | tf_op jit(solution)/shard_map/reduce_sum | solution.py:17
  88.7 8.7 %fusion.26 = f32[2048,768]{1,0:T(8,128)} fusion(bf16[768,768]{1,0:T(8,128)(2,1)S(1)} %copy-done, bf16[768,768]{1,0:T(8,128)(2,1)S(1)} %copy-done.7, bf16[2048,768]{1,0:T(8,128)(2,1)} %param.14, f32[768]{0:T(1024)S(1)} %copy-done.12, f32[2048]{0:T(1024)S(1)} %add_rsqrt_fusion.1), kind=kOutput, calls=%fused_computation.46 | convolution fusion | flops 4841275392 | bytes 11807744 | tf_op jit(solution)/shard_map/dot_general | solution.py:96
  97.4 13.2 %all-to-all-done.1 = bf16[3,32,24,768]{3,2,0,1:T(8,128)(2,1)} async-done(((bf16[3,32,24,768]{3,2,0,1:T(8,128)(2,1)}), bf16[3,32,24,768]{3,2,0,1:T(8,128)(2,1)}, u32[]{:S(2)}, u32[]{:S(2)}) %all-to-all-start.1) | async-done | bytes 3538976 | tf_op jit(solution)/shard_map/all_to_all | solution.py:74
  110.6 9.1 %all-to-all-start.3 = ((bf16[128,16,768]{2,1,0:T(8,128)(2,1)}), bf16[128,16,768]{2,1,0:T(8,128)(2,1)}, u32[]{:S(2)}, u32[]{:S(2)}) async-start(bf16[128,16,768]{2,1,0:T(8,128)(2,1)} %broadcast_select_fusion), calls=%async_computation.3 | async-start | bytes 6291456 | tf_op jit(solution)/shard_map/all_to_all | solution.py:160
  119.7 4.0 %copy.93 = bf16[3,32,24,768]{3,2,1,0:T(8,128)(2,1)} copy(bf16[3,32,24,768]{3,2,0,1:T(8,128)(2,1)} %all-to-all-done.1) | data formatting | bytes 7077888 | tf_op jit(solution)/shard_map/all_to_all | solution.py:74
  123.7 22.3 %multiply_reduce_fusion = (f32[2048]{0:T(1024)S(1)}, f32[2048,768]{1,0:T(8,128)}) fusion(f32[2048,768]{1,0:T(8,128)} %fusion.26, bf16[2304,768]{1,0:T(8,128)(2,1)} %bitcast.117, s32[]{:T(128)S(6)} %select_n.73, bf16[768,3072]{1,0:T(8,128)(2,1)} %all-gather.2.cloned.1.call-done, bf16[2048,768]{1,0:T(8,128)(2,1)} %param.14, f32[768]{0:T(1024)S(1)} %copy-done.12, ...), kind=kOutput, calls=%fused_computation.18 | convolution fusion | flops 14526183424 | bytes 27151364 | tf_op jit(solution)/shard_map/dot_general | solution.py:96
  146.1 3.8 %bitcast_reduce_fusion = f32[32,768]{1,0:T(8,128)S(1)} fusion(f32[2048,768]{1,0:T(8,128)} %get-tuple-element.72, f32[768]{0:T(1024)S(1)} %copy-done.10, f32[2048]{0:T(1024)S(1)} %add_rsqrt_fusion), kind=kLoop, calls=%fused_computation.16 | loop fusion | flops 4694016 | bytes 6401024 | tf_op jit(solution)/shard_map/reduce_sum | solution.py:101
  152.4 9.2 %all-to-all-done.3 = bf16[128,16,768]{2,1,0:T(8,128)(2,1)} async-done(((bf16[128,16,768]{2,1,0:T(8,128)(2,1)}), bf16[128,16,768]{2,1,0:T(8,128)(2,1)}, u32[]{:S(2)}, u32[]{:S(2)}) %all-to-all-start.3) | async-done | bytes 3145760 | tf_op jit(solution)/shard_map/all_to_all | solution.py:160
  161.6 3.8 %all-to-all-start.2 = ((bf16[128,2,896]{2,1,0:T(2,128)(2,1)}), bf16[128,2,896]{2,1,0:T(2,128)(2,1)S(1)}, u32[]{:S(2)}, u32[]{:S(2)}) async-start(bf16[128,2,896]{2,1,0:T(2,128)(2,1)} %all_to_all.28), calls=%async_computation.2 | async-start | bytes 917504 | tf_op jit(solution)/shard_map/all_to_all | solution.py:130
  165.4 4.6 %copy.103 = bf16[128,16,768]{2,0,1:T(8,128)(2,1)} copy(bf16[128,16,768]{2,1,0:T(8,128)(2,1)} %all-to-all-done.3) | data formatting | bytes 6291456 | tf_op jit(solution)/shard_map/all_to_all | solution.py:160
  169.9 8.8 %all-to-all-done.2 = bf16[128,2,896]{2,1,0:T(2,128)(2,1)S(1)} async-done(((bf16[128,2,896]{2,1,0:T(2,128)(2,1)}), bf16[128,2,896]{2,1,0:T(2,128)(2,1)S(1)}, u32[]{:S(2)}, u32[]{:S(2)}) %all-to-all-start.2) | async-done | bytes 458784 | tf_op jit(solution)/shard_map/all_to_all | solution.py:130
  184.1 2.3 fusion.8
  186.4 6.5 %copy.109 = bf16[128,16,896]{2,1,0:T(8,128)(2,1)} copy(bf16[128,16,896]{0,2,1:T(8,128)(2,1)} %bitcast.112) | data formatting | bytes 7340032 | tf_op jit(solution)/shard_map/all_to_all | solution.py:175
  192.9 4.8 %all-to-all-start.4 = ((bf16[128,16,896]{2,1,0:T(8,128)(2,1)}), bf16[128,16,896]{2,1,0:T(8,128)(2,1)}, u32[]{:S(2)}, u32[]{:S(2)}) async-start(bf16[128,16,896]{2,1,0:T(8,128)(2,1)} %copy.109), calls=%async_computation.4 | async-start | bytes 7340032 | tf_op jit(solution)/shard_map/all_to_all | solution.py:175
  198.1 47.2 %all-to-all-done.4 = bf16[128,16,896]{2,1,0:T(8,128)(2,1)} async-done(((bf16[128,16,896]{2,1,0:T(8,128)(2,1)}), bf16[128,16,896]{2,1,0:T(8,128)(2,1)}, u32[]{:S(2)}, u32[]{:S(2)}) %all-to-all-start.4) | async-done | bytes 3670048 | tf_op jit(solution)/shard_map/all_to_all | solution.py:175
  245.3 7.2 %gather_fusion.2 = bf16[1024,896]{1,0:T(8,128)(2,1)S(1)} fusion(bf16[2048,896]{1,0:T(8,128)(2,1)} %bitcast.53, s32[1024]{0:T(1024)S(1)} %broadcast_clamp_fusion), kind=kCustom, calls=%fused_computation.2 | custom fusion | bytes 3674112 | tf_op jit(solution)/shard_map/gather | solution.py:178
  (107 shorter events, 27.2 us)
Async XLA Ops:
  7.2 1.3 copy-start
  7.2 11.2 %copy-start.8 = (s32[32]{0:T(128)S(1)}, s32[32]{0:T(128)}, u32[]{:S(2)}) copy-start(s32[32]{0:T(128)} %param.20) | copy-start | bytes 388
  7.2 116.5 %all-gather.2.cloned.1.call-start = ((), (), s32[]{:S(2)}) async-start(), calls=%async_computation.5 | async-start | bytes 5898240 | tf_op jit(solution)/shard_map/all_gather | solution.py:82
  9.1 46.2 %all-to-all-start = ((bf16[4,24,768]{2,1,0:T(8,128)(2,1)}), bf16[4,24,768]{2,1,0:T(8,128)(2,1)S(1)}, u32[]{:S(2)}, u32[]{:S(2)}) async-start(bf16[4,24,768]{2,1,0:T(8,128)(2,1)} %broadcast_in_dim.55), calls=%async_computation | async-start | bytes 294912 | tf_op jit(solution)/shard_map/all_to_all | solution.py:65
  16.2 1.9 copy-start.3
  57.4 9.3 %copy-start.9 = (s32[128,8]{0,1:T(8,128)S(1)}, s32[128,8]{0,1:T(8,128)}, u32[]{:S(2)}) copy-start(s32[128,8]{0,1:T(8,128)} %param.22) | copy-start | bytes 12292
  57.4 53.2 %all-to-all-start.1 = ((bf16[3,32,24,768]{3,2,0,1:T(8,128)(2,1)}), bf16[3,32,24,768]{3,2,0,1:T(8,128)(2,1)}, u32[]{:S(2)}, u32[]{:S(2)}) async-start(bf16[3,32,24,768]{3,2,0,1:T(8,128)(2,1)} %broadcast_in_dim.56), calls=%async_computation.1 | async-start | bytes 7077888 | tf_op jit(solution)/shard_map/all_to_all | solution.py:74
  66.7 7.9 %copy-start.2 = (bf16[128,768]{1,0:T(8,128)(2,1)S(1)}, bf16[128,768]{1,0:T(8,128)(2,1)}, u32[]{:S(2)}) copy-start(bf16[128,768]{1,0:T(8,128)(2,1)} %param.21) | copy-start | bytes 589828
  84.0 2.8 %copy-start.5 = (bf16[2048,768]{1,0:T(8,128)(2,1)S(1)}, bf16[2048,768]{1,0:T(8,128)(2,1)}, u32[]{:S(2)}) copy-start(bf16[2048,768]{1,0:T(8,128)(2,1)} %gather_fusion.1) | copy-start | bytes 9437188
  86.7 1.9 copy-start.7
  86.8 1.9 copy-start.12
  110.6 51.0 %all-to-all-start.3 = ((bf16[128,16,768]{2,1,0:T(8,128)(2,1)}), bf16[128,16,768]{2,1,0:T(8,128)(2,1)}, u32[]{:S(2)}, u32[]{:S(2)}) async-start(bf16[128,16,768]{2,1,0:T(8,128)(2,1)} %broadcast_select_fusion), calls=%async_computation.3 | async-start | bytes 6291456 | tf_op jit(solution)/shard_map/all_to_all | solution.py:160
  123.7 22.4 %copy-start.10 = (f32[768]{0:T(1024)S(1)}, f32[768]{0:T(1024)}, u32[]{:S(2)}) copy-start(f32[768]{0:T(1024)} %param.18) | copy-start | bytes 9220
  161.6 17.1 %all-to-all-start.2 = ((bf16[128,2,896]{2,1,0:T(2,128)(2,1)}), bf16[128,2,896]{2,1,0:T(2,128)(2,1)S(1)}, u32[]{:S(2)}, u32[]{:S(2)}) async-start(bf16[128,2,896]{2,1,0:T(2,128)(2,1)} %all_to_all.28), calls=%async_computation.2 | async-start | bytes 917504 | tf_op jit(solution)/shard_map/all_to_all | solution.py:130
  179.2 2.5 copy-start.4
  181.6 2.2 copy-start.6
  192.9 4.8 %copy-start.11 = (s32[128]{0:T(128)S(1)}, s32[128]{0:T(128)}, u32[]{:S(2)}) copy-start(s32[128]{0:T(128)} %param.23) | copy-start | bytes 1540
  192.9 52.4 %all-to-all-start.4 = ((bf16[128,16,896]{2,1,0:T(8,128)(2,1)}), bf16[128,16,896]{2,1,0:T(8,128)(2,1)}, u32[]{:S(2)}, u32[]{:S(2)}) async-start(bf16[128,16,896]{2,1,0:T(8,128)(2,1)} %copy.109), calls=%async_computation.4 | async-start | bytes 7340032 | tf_op jit(solution)/shard_map/all_to_all | solution.py:175
  252.5 3.8 %copy-start.1 = (bf16[768,768]{1,0:T(8,128)(2,1)S(1)}, bf16[768,768]{1,0:T(8,128)(2,1)}, u32[]{:S(2)}) copy-start(bf16[768,768]{1,0:T(8,128)(2,1)} %param.16) | copy-start | bytes 3538948
Sparse Core Ops, SparseCore 0:
  9.7 55.4 all-gather.1

commit v3 on v2

--- a/solution.py
+++ b/solution.py
@@ -60,48 +60,31 @@
     piece_count = cache_count
     piece_rows = w_out.shape[0] // piece_count
     piece_at = lax.axis_index(CACHE) * piece_rows
-    mp_here = lax.axis_index("mp")
     own_piece = lax.dynamic_slice_in_dim(w_out, piece_at, piece_rows, axis=0)
-    mp_pieces = lax.all_to_all(
-        jnp.broadcast_to(own_piece[None], (mp_count,) + own_piece.shape),
-        "mp",
+    device_count = cache_count * mp_count
+    all_pieces = lax.all_to_all(
+        jnp.broadcast_to(own_piece[None], (device_count,) + own_piece.shape),
+        CACHE + ("mp",),
         split_axis=0,
         concat_axis=0,
         tiled=True,
     )
-    mp_twice = jnp.concatenate([mp_pieces, mp_pieces], axis=0)
-    other_pieces = lax.dynamic_slice_in_dim(mp_twice, mp_here + 1, mp_count - 1, axis=0)
-    rest_pieces = lax.all_to_all(
-        jnp.broadcast_to(other_pieces[:, None], (mp_count - 1, piece_count) + own_piece.shape),
-        CACHE,
-        split_axis=1,
-        concat_axis=1,
-        tiled=True,
-    )
-    w_out_rest = rest_pieces.reshape(-1, width)
+    w_out_all = all_pieces.reshape(-1, width)
     w_in_full = lax.all_gather(w_in, "mp", axis=1, tiled=True)
-    shard_cols = w_in.shape[1]
-    w_in_rest = lax.dynamic_slice_in_dim(
-        jnp.concatenate([w_in_full, w_in_full], axis=1),
-        (mp_here + 1) * shard_cols,
-        (mp_count - 1) * shard_cols,
-        axis=1,
-    )
-    hidden_own = jnp.maximum(
-        jnp.dot(normed, w_in, preferred_element_type=jnp.float32), 0.0
+    w_in_all = (
+        w_in_full.reshape(w_in.shape[0], mp_count, piece_count, piece_rows)
+        .transpose(0, 2, 1, 3)
+        .reshape(w_in.shape[0], -1)
+    )
+    hidden = jnp.maximum(
+        jnp.dot(normed, w_in_all, preferred_element_type=jnp.float32), 0.0
     ).astype(jnp.bfloat16)
-    hidden_rest = jnp.maximum(
-        jnp.dot(normed, w_in_rest, preferred_element_type=jnp.float32), 0.0
-    ).astype(jnp.bfloat16)
-    mixed = jnp.dot(hidden_own, w_out, preferred_element_type=jnp.float32) + jnp.dot(
-        hidden_rest, w_out_rest, preferred_element_type=jnp.float32
-    )
+    mixed = jnp.dot(hidden, w_out_all, preferred_element_type=jnp.float32)
     state_sum = tokens.astype(jnp.float32) + mixed
     final_rows = norm_rows(state_sum) * gain_out
     pooled = jnp.mean(final_rows.reshape(docs_here, doc_len, width), axis=1)
     embedded = norm_rows(pooled).astype(jnp.bfloat16)
     rows_own = stale_cache.shape[0]
-    device_count = cache_count * mp_count
     refresh_cap = 2 * docs_here // cache_count
     dest_of = refresh_ids // rows_own
     dest_hits = (dest_of[:, None] == jnp.arange(device_count, dtype=jnp.int32)[None, :]).astype(

time: 264 us -> 272 us (1.030)
  waiting for transfers between devices: 79.1 us -> 98.2 us
  matrix products: 36.3 us -> 30.5 us
  starting transfers between devices: 31.9 us -> 27.4 us
    all_gather x1, waiting for transfers between devices: 0.01 us -> 32.6 us  [shards(): w_in_full = lax.all_gather(w_in, 'mp', axis=1, tiled=True)]
    all_to_all x2 -> x1, waiting for transfers between devices: 13.2 us -> 1.47 us  [shards(): lax.all_to_all(jnp.broadcast_to(own_piece[None], (device_count,) + own_pi...]
    transpose x0 -> x1, local copies, waits for them, and re-layouts: none -> 5.1 us  [shards(): w_in_all = w_in_full.reshape(w_in.shape[0], mp_count, piece_count, piece_...]
    dot_general x2 -> x1, matrix products: 31 us -> 26.7 us  [shards(): mixed = jnp.dot(hidden, w_out_all, preferred_element_type=jnp.float32)]
    all_to_all x1 -> x0, local copies, waits for them, and re-layouts: 3.99 us -> none  [shards(): lax.all_to_all(jnp.broadcast_to(other_pieces[:, None], (mp_count - 1, pie...]
    unnamed x30 -> x31, local copies, waits for them, and re-layouts: 3.53 us -> 5.83 us
    all_to_all x2 -> x1, starting transfers between devices: 14.1 us -> 11.9 us  [shards(): lax.all_to_all(jnp.broadcast_to(own_piece[None], (device_count,) + own_pi...]
  transfers between devices with their start and end apart: 6 -> 5, of which waited for: 4 -> 5; matrix products, arithmetic and copies ran while one was open for 41% -> 37% of each run, Pallas kernels for 0% -> 0%
where the time goes in v3:
time: 272 us; the launch traced here: 271 us
  waiting for transfers between devices  98.2 us (36%)
  local copies, waits for them, and re-layouts  55.7 us (20%)
  other arithmetic  44.4 us (16%)
  matrix products  30.5 us (11%)
  starting transfers between devices  27.4 us (10%)
  between operations  14.5 us (5%)
    all_to_all x1, waiting for transfers between devices, shards(): lax.all_to_all(packed.reshape(-1, packed.shape[-1]), CACHE + ('mp',), spl...  47.2 us
    all_gather x1, waiting for transfers between devices, shards(): w_in_full = lax.all_gather(w_in, 'mp', axis=1, tiled=True)  32.6 us
    dot_general x1, matrix products, shards(): mixed = jnp.dot(hidden, w_out_all, preferred_element_type=jnp.float32)  26.7 us
    another operation x6, other arithmetic  23.3 us
    all_to_all x1, starting transfers between devices, shards(): lax.all_to_all(jnp.broadcast_to(own_piece[None], (device_count,) + own_pi...  11.9 us
    gather x1, local copies, waits for them, and re-layouts, shards(): queries[jnp.maximum(slot_pair, 0) // neg_count]  9.39 us
    all_to_all x1, waiting for transfers between devices, shards(): lax.all_to_all(out_rows, CACHE + ('mp',), split_axis=0, concat_axis=0, ti...  8.64 us
    all_to_all x1, waiting for transfers between devices, shards(): lax.all_to_all(outbound, CACHE + ('mp',), split_axis=0, concat_axis=0, ti...  8.24 us
  transfers between devices with their start and end apart: 5, of which 5 were waited for; matrix products, arithmetic and copies ran while one was open for 37% of the time, Pallas kernels for 0%

profile of v3, /device:TPU:1, one launch (start us, length us, event | category | flops | bytes accessed | tf_op | source)
XLA Modules:
  0.0 270.7 jit_solution(10097964184669171154)
XLA Ops:
  7.2 2.5 copy.89
  9.7 2.5 broadcast_in_dim.53
  12.3 11.9 %all-to-all-start = ((bf16[128,24,768]{2,1,0:T(8,128)(2,1)}), bf16[128,24,768]{2,1,0:T(8,128)(2,1)}, u32[]{:S(2)}, u32[]{:S(2)}) async-start(bf16[128,24,768]{2,1,0:T(8,128)(2,1)} %broadcast_in_dim.53), calls=%async_computation | async-start | bytes 9437184 | tf_op jit(solution)/shard_map/all_to_all | solution.py:65
  28.2 20.9 %fusion.42 = (f32[256]{0:T(256)S(1)}, s32[256]{0:T(256)S(1)}, pred[256]{0:T(512)(128)(4,1)S(1)}) fusion(pred[]{:T(512)} %compare_reduce_fusion, s32[]{:T(128)} %bitcast.36, s32[]{:T(128)} %bitcast.35, s32[]{:T(128)} %bitcast.34, s32[]{:T(128)} %bitcast.33, s32[]{:T(128)} %bitcast.32, s32[]{:T(128)} %bitcast.31, s32[]{:T(128)} %bitcast.30, s32[]{:T(128)} %bitcast.29, ...), kind=kLoop, calls=%fused_computation.150 | loop fusion | flops 23040 | bytes 3457 | tf_op jit(solution)/shard_map/select.23
  52.6 2.7 add_add_fusion
  55.3 4.4 %copy.99 = s32[1024,8,128]{0,2,1:T(8,128)} copy(s32[1024,8,128]{0,1,2:T(8,128)S(1)} %add_add_fusion) | data formatting | bytes 8388608 | tf_op jit(solution)/shard_map/sub | solution.py:131
  59.9 2.9 %fusion.5 = s32[1024]{0:T(1024)S(1)} fusion(s32[1024,8,128]{0,2,1:T(8,128)} %copy.99, s32[1024]{0:T(1024)S(1)} %eq.73), kind=kLoop, calls=%fused_computation.19 | loop fusion | flops 3144704 | bytes 4202496 | tf_op jit(solution)/shard_map/reduce_sum | solution.py:131
  62.9 4.3 %scatter_custom_fusion.1 = s32[2048]{0:T(1024)S(1)} fusion(s32[1024]{0:T(1024)S(1)} %bitcast.123, s32[1024]{0:T(1024)S(1)} %iota.37, s32[]{:T(128)} %constant.162.clone.1), kind=kCustom, calls=%fused_computation.97 | custom fusion | bytes 8196 | tf_op jit(solution)/shard_map/scatter | solution.py:136
  67.4 9.4 %gather_fusion.1 = bf16[2048,768]{1,0:T(8,128)(2,1)} fusion(bf16[128,768]{1,0:T(8,128)(2,1)S(1)} %copy-done.2, s32[2048]{0:T(1024)S(1)} %fusion.35), kind=kCustom, calls=%fused_computation.1 | custom fusion | bytes 6299648 | tf_op jit(solution)/shard_map/gather | solution.py:140
  77.0 2.7 %fusion.1 = f32[2048]{0:T(1024)S(1)} fusion(bf16[2048,768]{1,0:T(8,128)(2,1)} %param.14), kind=kLoop, calls=%fused_computation.11 | loop fusion | flops 4716544 | bytes 3153920 | tf_op jit(solution)/shard_map/reduce_sum | solution.py:17
  81.7 32.6 %all-gather.2.cloned.1.call-done = bf16[768,3072]{0,1:T(8,128)(2,1)} async-done(((bf16[768,768]{0,1:T(8,128)(2,1)}), bf16[768,3072]{0,1:T(8,128)(2,1)}) %all-gather.2.cloned.1.call-update) | async-done | bytes 4718608 | tf_op jit(solution)/shard_map/all_gather | solution.py:73
  114.3 5.1 %copy.90 = bf16[768,32,4,24]{0,3,2,1:T(8,128)(2,1)} copy(bf16[768,32,4,24]{0,3,1,2:T(8,128)(2,1)} %bitcast.120) | data formatting | bytes 9437184 | tf_op jit(solution)/shard_map/transpose | solution.py:76
  120.9 6.9 %all-to-all-start.2 = ((bf16[128,16,768]{2,1,0:T(8,128)(2,1)}), bf16[128,16,768]{2,1,0:T(8,128)(2,1)}, u32[]{:S(2)}, u32[]{:S(2)}) async-start(bf16[128,16,768]{2,1,0:T(8,128)(2,1)} %broadcast_select_fusion), calls=%async_computation.2 | async-start | bytes 6291456 | tf_op jit(solution)/shard_map/all_to_all | solution.py:143
  127.8 26.7 %multiply_reduce_fusion = (f32[2048]{0:T(1024)S(1)}, f32[2048,768]{1,0:T(8,128)}) fusion(bf16[2048,768]{1,0:T(8,128)(2,1)} %param.14, bf16[3072,768]{1,0:T(8,128)(2,1)} %bitcast.3, bf16[768,3072]{0,1:T(8,128)(2,1)} %bitcast.121, f32[768]{0:T(1024)S(1)} %copy-done.12, f32[2048]{0:T(1024)S(1)} %add_rsqrt_fusion.1), kind=kOutput, calls=%fused_computation.16 | convolution fusion | flops 19352516608 | bytes 18893824 | tf_op jit(solution)/shard_map/dot_general | solution.py:82
  154.5 4.4 %bitcast_reduce_fusion = f32[32,768]{1,0:T(8,128)S(1)} fusion(f32[2048,768]{1,0:T(8,128)} %get-tuple-element.72, bf16[2048,768]{1,0:T(8,128)(2,1)} %param.14, f32[768]{0:T(1024)S(1)} %copy-done.9, f32[2048]{0:T(1024)S(1)} %add_rsqrt_fusion), kind=kLoop, calls=%fused_computation.14 | loop fusion | flops 7839744 | bytes 9546752 | tf_op jit(solution)/shard_map/reduce_sum | solution.py:85
  161.4 8.2 %all-to-all-done.2 = bf16[128,16,768]{2,1,0:T(8,128)(2,1)} async-done(((bf16[128,16,768]{2,1,0:T(8,128)(2,1)}), bf16[128,16,768]{2,1,0:T(8,128)(2,1)}, u32[]{:S(2)}, u32[]{:S(2)}) %all-to-all-start.2) | async-done | bytes 3145760 | tf_op jit(solution)/shard_map/all_to_all | solution.py:143
  169.7 3.8 %all-to-all-start.1 = ((bf16[128,2,896]{2,1,0:T(2,128)(2,1)}), bf16[128,2,896]{2,1,0:T(2,128)(2,1)S(1)}, u32[]{:S(2)}, u32[]{:S(2)}) async-start(bf16[128,2,896]{2,1,0:T(2,128)(2,1)} %all_to_all.24), calls=%async_computation.1 | async-start | bytes 917504 | tf_op jit(solution)/shard_map/all_to_all | solution.py:113
  173.4 4.7 %copy.100 = bf16[128,16,768]{2,0,1:T(8,128)(2,1)} copy(bf16[128,16,768]{2,1,0:T(8,128)(2,1)} %all-to-all-done.2) | data formatting | bytes 6291456 | tf_op jit(solution)/shard_map/all_to_all | solution.py:143
  178.1 8.6 %all-to-all-done.1 = bf16[128,2,896]{2,1,0:T(2,128)(2,1)S(1)} async-done(((bf16[128,2,896]{2,1,0:T(2,128)(2,1)}), bf16[128,2,896]{2,1,0:T(2,128)(2,1)S(1)}, u32[]{:S(2)}, u32[]{:S(2)}) %all-to-all-start.1) | async-done | bytes 458784 | tf_op jit(solution)/shard_map/all_to_all | solution.py:113
  191.7 2.3 fusion.8
  193.9 6.5 %copy.106 = bf16[128,16,896]{2,1,0:T(8,128)(2,1)} copy(bf16[128,16,896]{0,2,1:T(8,128)(2,1)} %bitcast.115) | data formatting | bytes 7340032 | tf_op jit(solution)/shard_map/all_to_all | solution.py:158
  200.4 4.8 %all-to-all-start.3 = ((bf16[128,16,896]{2,1,0:T(8,128)(2,1)}), bf16[128,16,896]{2,1,0:T(8,128)(2,1)}, u32[]{:S(2)}, u32[]{:S(2)}) async-start(bf16[128,16,896]{2,1,0:T(8,128)(2,1)} %copy.106), calls=%async_computation.3 | async-start | bytes 7340032 | tf_op jit(solution)/shard_map/all_to_all | solution.py:158
  205.6 47.2 %all-to-all-done.3 = bf16[128,16,896]{2,1,0:T(8,128)(2,1)} async-done(((bf16[128,16,896]{2,1,0:T(8,128)(2,1)}), bf16[128,16,896]{2,1,0:T(8,128)(2,1)}, u32[]{:S(2)}, u32[]{:S(2)}) %all-to-all-start.3) | async-done | bytes 3670048 | tf_op jit(solution)/shard_map/all_to_all | solution.py:158
  252.9 7.2 %gather_fusion.2 = bf16[1024,896]{1,0:T(8,128)(2,1)S(1)} fusion(bf16[2048,896]{1,0:T(8,128)(2,1)} %bitcast.56, s32[1024]{0:T(1024)S(1)} %broadcast_clamp_fusion), kind=kCustom, calls=%fused_computation.2 | custom fusion | bytes 3674112 | tf_op jit(solution)/shard_map/gather | solution.py:161
  (103 shorter events, 23.0 us)
Async XLA Ops:
  7.2 2.6 copy-start
  7.2 107.1 %all-gather.2.cloned.1.call-start = ((), (), s32[]{:S(2)}) async-start(), calls=%async_computation.4 | async-start | bytes 5898240 | tf_op jit(solution)/shard_map/all_gather | solution.py:73
  12.3 11.9 %copy-start.7 = (s32[32]{0:T(128)S(1)}, s32[32]{0:T(128)}, u32[]{:S(2)}) copy-start(s32[32]{0:T(128)} %param.20) | copy-start | bytes 388
  12.3 12.0 %copy-start.8 = (s32[128,8]{0,1:T(8,128)S(1)}, s32[128,8]{0,1:T(8,128)}, u32[]{:S(2)}) copy-start(s32[128,8]{0,1:T(8,128)} %param.22) | copy-start | bytes 12292
  12.3 108.6 %all-to-all-start = ((bf16[128,24,768]{2,1,0:T(8,128)(2,1)}), bf16[128,24,768]{2,1,0:T(8,128)(2,1)}, u32[]{:S(2)}, u32[]{:S(2)}) async-start(bf16[128,24,768]{2,1,0:T(8,128)(2,1)} %broadcast_in_dim.53), calls=%async_computation | async-start | bytes 9437184 | tf_op jit(solution)/shard_map/all_to_all | solution.py:65
  50.6 1.9 copy-start.3
  59.7 7.7 %copy-start.2 = (bf16[128,768]{1,0:T(8,128)(2,1)S(1)}, bf16[128,768]{1,0:T(8,128)(2,1)}, u32[]{:S(2)}) copy-start(bf16[128,768]{1,0:T(8,128)(2,1)} %param.21) | copy-start | bytes 589828
  77.0 2.8 %copy-start.5 = (bf16[2048,768]{1,0:T(8,128)(2,1)S(1)}, bf16[2048,768]{1,0:T(8,128)(2,1)}, u32[]{:S(2)}) copy-start(bf16[2048,768]{1,0:T(8,128)(2,1)} %gather_fusion.1) | copy-start | bytes 9437188
  119.4 8.4 %copy-start.12 = (f32[768]{0:T(1024)S(1)}, f32[768]{0:T(1024)}, u32[]{:S(2)}) copy-start(f32[768]{0:T(1024)} %param.17) | copy-start | bytes 9220
  120.9 48.8 %all-to-all-start.2 = ((bf16[128,16,768]{2,1,0:T(8,128)(2,1)}), bf16[128,16,768]{2,1,0:T(8,128)(2,1)}, u32[]{:S(2)}, u32[]{:S(2)}) async-start(bf16[128,16,768]{2,1,0:T(8,128)(2,1)} %broadcast_select_fusion), calls=%async_computation.2 | async-start | bytes 6291456 | tf_op jit(solution)/shard_map/all_to_all | solution.py:143
  127.8 26.7 %copy-start.9 = (f32[768]{0:T(1024)S(1)}, f32[768]{0:T(1024)}, u32[]{:S(2)}) copy-start(f32[768]{0:T(1024)} %param.18) | copy-start | bytes 9220
  169.7 17.1 %all-to-all-start.1 = ((bf16[128,2,896]{2,1,0:T(2,128)(2,1)}), bf16[128,2,896]{2,1,0:T(2,128)(2,1)S(1)}, u32[]{:S(2)}, u32[]{:S(2)}) async-start(bf16[128,2,896]{2,1,0:T(2,128)(2,1)} %all_to_all.24), calls=%async_computation.1 | async-start | bytes 917504 | tf_op jit(solution)/shard_map/all_to_all | solution.py:113
  173.4 14.0 %copy-start.11 = (bf16[1024,768]{1,0:T(8,128)(2,1)S(1)}, bf16[1024,768]{1,0:T(8,128)(2,1)}, u32[]{:S(2)}) copy-start(bf16[1024,768]{1,0:T(8,128)(2,1)} %param.19) | copy-start | bytes 4718596
  187.2 2.0 copy-start.4
  188.1 3.2 %copy-start.6 = (bf16[1024,768]{1,0:T(8,128)(2,1)}, bf16[1024,768]{1,0:T(8,128)(2,1)S(1)}, u32[]{:S(2)}) copy-start(bf16[1024,768]{1,0:T(8,128)(2,1)S(1)} %broadcast_select_fusion.1) | copy-start | bytes 4718596
  200.4 4.8 %copy-start.10 = (s32[128]{0:T(128)S(1)}, s32[128]{0:T(128)}, u32[]{:S(2)}) copy-start(s32[128]{0:T(128)} %param.23) | copy-start | bytes 1540
  200.4 52.4 %all-to-all-start.3 = ((bf16[128,16,896]{2,1,0:T(8,128)(2,1)}), bf16[128,16,896]{2,1,0:T(8,128)(2,1)}, u32[]{:S(2)}, u32[]{:S(2)}) async-start(bf16[128,16,896]{2,1,0:T(8,128)(2,1)} %copy.106), calls=%async_computation.3 | async-start | bytes 7340032 | tf_op jit(solution)/shard_map/all_to_all | solution.py:158
  260.0 3.8 %copy-start.1 = (bf16[768,768]{1,0:T(8,128)(2,1)S(1)}, bf16[768,768]{1,0:T(8,128)(2,1)}, u32[]{:S(2)}) copy-start(bf16[768,768]{1,0:T(8,128)(2,1)} %param.16) | copy-start | bytes 3538948
Sparse Core Ops, SparseCore 0:
  10.2 104.0 all-gather.1

commit v4 on v2

--- a/solution.py
+++ b/solution.py
@@ -69,6 +69,7 @@
         concat_axis=0,
         tiled=True,
     )
+    normed, mp_pieces = lax.optimization_barrier((normed, mp_pieces))
     mp_twice = jnp.concatenate([mp_pieces, mp_pieces], axis=0)
     other_pieces = lax.dynamic_slice_in_dim(mp_twice, mp_here + 1, mp_count - 1, axis=0)
     rest_pieces = lax.all_to_all(

time: 264 us -> 260 us (0.985)
  waiting for transfers between devices: 79.1 us -> 72.6 us
    all_to_all x1, waiting for transfers between devices: 13.2 us -> 6.29 us  [shards(): lax.all_to_all(jnp.broadcast_to(other_pieces[:, None], (mp_count - 1, pie...]
  transfers between devices with their start and end apart: 6 -> 6, of which waited for: 4 -> 4; matrix products, arithmetic and copies ran while one was open for 41% -> 43% of each run, Pallas kernels for 0% -> 0%
where the time goes in v4:
time: 260 us; the launch traced here: 259 us
  waiting for transfers between devices  72.6 us (28%)
  local copies, waits for them, and re-layouts  54.9 us (21%)
  other arithmetic  49.4 us (19%)
  matrix products  36 us (14%)
  starting transfers between devices  31.7 us (12%)
  between operations  14.5 us (6%)
    all_to_all x1, waiting for transfers between devices, shards(): lax.all_to_all(packed.reshape(-1, packed.shape[-1]), CACHE + ('mp',), spl...  47.2 us
    another operation x6, other arithmetic  23.2 us
    dot_general x1, matrix products, shards(): jnp.dot(hidden_rest, w_out_rest, preferred_element_type=jnp.float32)  22.1 us
    all_to_all x1, waiting for transfers between devices, shards(): lax.all_to_all(outbound, CACHE + ('mp',), split_axis=0, concat_axis=0, ti...  9.45 us
    gather x1, local copies, waits for them, and re-layouts, shards(): queries[jnp.maximum(slot_pair, 0) // neg_count]  9.38 us
    all_to_all x1, starting transfers between devices, shards(): lax.all_to_all(outbound, CACHE + ('mp',), split_axis=0, concat_axis=0, ti...  9.26 us
    all_to_all x1, waiting for transfers between devices, shards(): lax.all_to_all(out_rows, CACHE + ('mp',), split_axis=0, concat_axis=0, ti...  8.98 us
    all_to_all x1, starting transfers between devices, shards(): lax.all_to_all(jnp.broadcast_to(other_pieces[:, None], (mp_count - 1, pie...  8.92 us
  transfers between devices with their start and end apart: 6, of which 4 were waited for; matrix products, arithmetic and copies ran while one was open for 43% of the time, Pallas kernels for 0%

profile of v4, /device:TPU:1, one launch (start us, length us, event | category | flops | bytes accessed | tf_op | source)
XLA Modules:
  0.0 259.0 jit_solution(3981317167142914774)
XLA Ops:
  9.1 4.8 %all-to-all-start = ((bf16[4,24,768]{2,1,0:T(8,128)(2,1)}), bf16[4,24,768]{2,1,0:T(8,128)(2,1)S(1)}, u32[]{:S(2)}, u32[]{:S(2)}) async-start(bf16[4,24,768]{2,1,0:T(8,128)(2,1)} %broadcast_in_dim.55), calls=%async_computation | async-start | bytes 294912 | tf_op jit(solution)/shard_map/all_to_all | solution.py:65
  21.8 3.1 %fusion.1 = f32[2048]{0:T(1024)S(1)} fusion(bf16[2048,768]{1,0:T(8,128)(2,1)} %param.14), kind=kLoop, calls=%fused_computation.13 | loop fusion | flops 4716544 | bytes 3153920 | tf_op jit(solution)/shard_map/reduce_sum | solution.py:17
  29.8 20.8 %fusion.45 = (f32[256]{0:T(256)S(1)}, s32[256]{0:T(256)S(1)}, pred[256]{0:T(512)(128)(4,1)S(1)}) fusion(pred[]{:T(512)} %compare_reduce_fusion, s32[]{:T(128)} %bitcast.33, s32[]{:T(128)} %bitcast.32, s32[]{:T(128)} %bitcast.31, s32[]{:T(128)} %bitcast.30, s32[]{:T(128)} %bitcast.29, s32[]{:T(128)} %bitcast.28, s32[]{:T(128)} %bitcast.27, s32[]{:T(128)} %bitcast.26, ...), kind=kLoop, calls=%fused_computation.158 | loop fusion | flops 23040 | bytes 3457 | tf_op jit(solution)/shard_map/select.23
  53.2 8.9 %all-to-all-start.1 = ((bf16[3,32,24,768]{3,2,0,1:T(8,128)(2,1)}), bf16[3,32,24,768]{3,2,0,1:T(8,128)(2,1)}, u32[]{:S(2)}, u32[]{:S(2)}) async-start(bf16[3,32,24,768]{3,2,0,1:T(8,128)(2,1)} %broadcast_in_dim.56), calls=%async_computation.1 | async-start | bytes 7077888 | tf_op jit(solution)/shard_map/all_to_all | solution.py:75
  63.3 2.7 %add_add_fusion = s32[1024,8,128]{0,1,2:T(8,128)S(1)} fusion(s32[1024,8,128]{0,1,2:T(8,128)} %copy-done.3, s32[1024,8]{0,1:T(8,128)S(1)} %slice.128), kind=kLoop, calls=%fused_computation.23 | loop fusion | flops 2097152 | bytes 8421376 | tf_op jit(solution)/shard_map/sub | solution.py:149
  66.0 4.4 %copy.102 = s32[1024,8,128]{0,2,1:T(8,128)} copy(s32[1024,8,128]{0,1,2:T(8,128)S(1)} %add_add_fusion) | data formatting | bytes 8388608 | tf_op jit(solution)/shard_map/sub | solution.py:149
  70.5 2.9 %fusion.5 = s32[1024]{0:T(1024)S(1)} fusion(s32[1024,8,128]{0,2,1:T(8,128)} %copy.102, s32[1024]{0:T(1024)S(1)} %eq.73), kind=kLoop, calls=%fused_computation.22 | loop fusion | flops 3144704 | bytes 4202496 | tf_op jit(solution)/shard_map/reduce_sum | solution.py:149
  73.5 4.3 %scatter_custom_fusion.1 = s32[2048]{0:T(1024)S(1)} fusion(s32[1024]{0:T(1024)S(1)} %bitcast.121, s32[1024]{0:T(1024)S(1)} %iota.37, s32[]{:T(128)} %constant.168.clone.1), kind=kCustom, calls=%fused_computation.103 | custom fusion | bytes 8196 | tf_op jit(solution)/shard_map/scatter | solution.py:154
  78.4 9.4 %gather_fusion.1 = bf16[2048,768]{1,0:T(8,128)(2,1)} fusion(bf16[128,768]{1,0:T(8,128)(2,1)S(1)} %copy-done.2, s32[2048]{0:T(1024)S(1)} %fusion.36), kind=kCustom, calls=%fused_computation.1 | custom fusion | bytes 6299648 | tf_op jit(solution)/shard_map/gather | solution.py:158
  87.8 3.4 %broadcast_select_fusion = bf16[128,16,768]{2,1,0:T(8,128)(2,1)} fusion(bf16[128,16,768]{2,1,0:T(8,128)(2,1)} %bitcast.116, pred[128,16]{1,0:T(8,128)(4,1)S(1)} %broadcast_in_dim.98), kind=kLoop, calls=%fused_computation.31 | loop fusion | flops 1572864 | bytes 6293504 | tf_op jit(solution)/shard_map/jit(_where)/select_n | solution.py:156
  91.2 8.6 %fusion.19 = f32[2048,768]{1,0:T(8,128)} fusion(bf16[768,768]{1,0:T(8,128)(2,1)S(1)} %copy-done, bf16[2048,768]{1,0:T(8,128)(2,1)} %fusion.3, bf16[768,768]{1,0:T(8,128)(2,1)S(1)} %copy-done.7), kind=kOutput, calls=%fused_computation.44 | convolution fusion | flops 4834983936 | bytes 11796480 | tf_op jit(solution)/shard_map/dot_general | solution.py:97
  99.8 6.3 %all-to-all-done.1 = bf16[3,32,24,768]{3,2,0,1:T(8,128)(2,1)} async-done(((bf16[3,32,24,768]{3,2,0,1:T(8,128)(2,1)}), bf16[3,32,24,768]{3,2,0,1:T(8,128)(2,1)}, u32[]{:S(2)}, u32[]{:S(2)}) %all-to-all-start.1) | async-done | bytes 3538976 | tf_op jit(solution)/shard_map/all_to_all | solution.py:75
  106.1 9.3 %all-to-all-start.3 = ((bf16[128,16,768]{2,1,0:T(8,128)(2,1)}), bf16[128,16,768]{2,1,0:T(8,128)(2,1)}, u32[]{:S(2)}, u32[]{:S(2)}) async-start(bf16[128,16,768]{2,1,0:T(8,128)(2,1)} %broadcast_select_fusion), calls=%async_computation.3 | async-start | bytes 6291456 | tf_op jit(solution)/shard_map/all_to_all | solution.py:161
  115.4 4.0 %copy.93 = bf16[3,32,24,768]{3,2,1,0:T(8,128)(2,1)} copy(bf16[3,32,24,768]{3,2,0,1:T(8,128)(2,1)} %all-to-all-done.1) | data formatting | bytes 7077888 | tf_op jit(solution)/shard_map/all_to_all | solution.py:75
  119.4 22.1 %multiply_reduce_fusion = (f32[2048]{0:T(1024)S(1)}, f32[2048,768]{1,0:T(8,128)}) fusion(f32[2048,768]{1,0:T(8,128)} %fusion.19, bf16[2304,768]{1,0:T(8,128)(2,1)} %bitcast.119, bf16[2048,768]{1,0:T(8,128)(2,1)} %fusion.3, s32[]{:T(128)S(6)} %select_n.74, bf16[768,3072]{1,0:T(8,128)(2,1)} %all-gather.2.cloned.1.call-done, bf16[2048,768]{1,0:T(8,128)(2,1)} %param.14), kind=kOutput, calls=%fused_computation.18 | convolution fusion | flops 14519891968 | bytes 27140100 | tf_op jit(solution)/shard_map/dot_general | solution.py:97
  141.5 3.8 %bitcast_reduce_fusion = f32[32,768]{1,0:T(8,128)S(1)} fusion(f32[2048,768]{1,0:T(8,128)} %get-tuple-element.76, f32[768]{0:T(1024)S(1)} %copy-done.10, f32[2048]{0:T(1024)S(1)} %add_rsqrt_fusion), kind=kLoop, calls=%fused_computation.16 | loop fusion | flops 4694016 | bytes 6401024 | tf_op jit(solution)/shard_map/reduce_sum | solution.py:102
  147.8 9.4 %all-to-all-done.3 = bf16[128,16,768]{2,1,0:T(8,128)(2,1)} async-done(((bf16[128,16,768]{2,1,0:T(8,128)(2,1)}), bf16[128,16,768]{2,1,0:T(8,128)(2,1)}, u32[]{:S(2)}, u32[]{:S(2)}) %all-to-all-start.3) | async-done | bytes 3145760 | tf_op jit(solution)/shard_map/all_to_all | solution.py:161
  157.3 3.8 %all-to-all-start.2 = ((bf16[128,2,896]{2,1,0:T(2,128)(2,1)}), bf16[128,2,896]{2,1,0:T(2,128)(2,1)S(1)}, u32[]{:S(2)}, u32[]{:S(2)}) async-start(bf16[128,2,896]{2,1,0:T(2,128)(2,1)} %all_to_all.28), calls=%async_computation.2 | async-start | bytes 917504 | tf_op jit(solution)/shard_map/all_to_all | solution.py:131
  161.1 4.6 %copy.103 = bf16[128,16,768]{2,0,1:T(8,128)(2,1)} copy(bf16[128,16,768]{2,1,0:T(8,128)(2,1)} %all-to-all-done.3) | data formatting | bytes 6291456 | tf_op jit(solution)/shard_map/all_to_all | solution.py:161
  165.6 9.0 %all-to-all-done.2 = bf16[128,2,896]{2,1,0:T(2,128)(2,1)S(1)} async-done(((bf16[128,2,896]{2,1,0:T(2,128)(2,1)}), bf16[128,2,896]{2,1,0:T(2,128)(2,1)S(1)}, u32[]{:S(2)}, u32[]{:S(2)}) %all-to-all-start.2) | async-done | bytes 458784 | tf_op jit(solution)/shard_map/all_to_all | solution.py:131
  182.3 6.5 %copy.109 = bf16[128,16,896]{2,1,0:T(8,128)(2,1)} copy(bf16[128,16,896]{0,2,1:T(8,128)(2,1)} %bitcast.114) | data formatting | bytes 7340032 | tf_op jit(solution)/shard_map/all_to_all | solution.py:176
  188.8 4.8 %all-to-all-start.4 = ((bf16[128,16,896]{2,1,0:T(8,128)(2,1)}), bf16[128,16,896]{2,1,0:T(8,128)(2,1)}, u32[]{:S(2)}, u32[]{:S(2)}) async-start(bf16[128,16,896]{2,1,0:T(8,128)(2,1)} %copy.109), calls=%async_computation.4 | async-start | bytes 7340032 | tf_op jit(solution)/shard_map/all_to_all | solution.py:176
  194.0 47.2 %all-to-all-done.4 = bf16[128,16,896]{2,1,0:T(8,128)(2,1)} async-done(((bf16[128,16,896]{2,1,0:T(8,128)(2,1)}), bf16[128,16,896]{2,1,0:T(8,128)(2,1)}, u32[]{:S(2)}, u32[]{:S(2)}) %all-to-all-start.4) | async-done | bytes 3670048 | tf_op jit(solution)/shard_map/all_to_all | solution.py:176
  241.2 7.2 %gather_fusion.2 = bf16[1024,896]{1,0:T(8,128)(2,1)S(1)} fusion(bf16[2048,896]{1,0:T(8,128)(2,1)} %bitcast.53, s32[1024]{0:T(1024)S(1)} %broadcast_clamp_fusion), kind=kCustom, calls=%fused_computation.2 | custom fusion | bytes 3674112 | tf_op jit(solution)/shard_map/gather | solution.py:179
  (106 shorter events, 33.3 us)
Async XLA Ops:
  7.2 1.3 copy-start
  7.2 112.2 %all-gather.2.cloned.1.call-start = ((), (), s32[]{:S(2)}) async-start(), calls=%async_computation.5 | async-start | bytes 5898240 | tf_op jit(solution)/shard_map/all_gather | solution.py:83
  9.1 42.1 %all-to-all-start = ((bf16[4,24,768]{2,1,0:T(8,128)(2,1)}), bf16[4,24,768]{2,1,0:T(8,128)(2,1)S(1)}, u32[]{:S(2)}, u32[]{:S(2)}) async-start(bf16[4,24,768]{2,1,0:T(8,128)(2,1)} %broadcast_in_dim.55), calls=%async_computation | async-start | bytes 294912 | tf_op jit(solution)/shard_map/all_to_all | solution.py:65
  21.8 5.6 %copy-start.4 = (bf16[2048,768]{1,0:T(8,128)(2,1)S(1)}, bf16[2048,768]{1,0:T(8,128)(2,1)}, u32[]{:S(2)}) copy-start(bf16[2048,768]{1,0:T(8,128)(2,1)} %param.14) | copy-start | bytes 9437188
  21.8 5.5 %copy-start.9 = (f32[768]{0:T(1024)S(1)}, f32[768]{0:T(1024)}, u32[]{:S(2)}) copy-start(f32[768]{0:T(1024)} %param.17) | copy-start | bytes 9220
  25.4 1.9 copy-start.3
  53.2 52.9 %all-to-all-start.1 = ((bf16[3,32,24,768]{3,2,0,1:T(8,128)(2,1)}), bf16[3,32,24,768]{3,2,0,1:T(8,128)(2,1)}, u32[]{:S(2)}, u32[]{:S(2)}) async-start(bf16[3,32,24,768]{3,2,0,1:T(8,128)(2,1)} %broadcast_in_dim.56), calls=%async_computation.1 | async-start | bytes 7077888 | tf_op jit(solution)/shard_map/all_to_all | solution.py:75
  65.9 4.4 %copy-start.8 = (s32[128,8]{0,1:T(8,128)S(1)}, s32[128,8]{0,1:T(8,128)}, u32[]{:S(2)}) copy-start(s32[128,8]{0,1:T(8,128)} %param.22) | copy-start | bytes 12292
  70.3 8.1 %copy-start.2 = (bf16[128,768]{1,0:T(8,128)(2,1)S(1)}, bf16[128,768]{1,0:T(8,128)(2,1)}, u32[]{:S(2)}) copy-start(bf16[128,768]{1,0:T(8,128)(2,1)} %param.21) | copy-start | bytes 589828
  87.8 3.4 %copy-start.7 = (bf16[768,768]{1,0:T(8,128)(2,1)S(1)}, bf16[768,768]{1,0:T(8,128)(2,1)}, u32[]{:S(2)}) copy-start(bf16[768,768]{1,0:T(8,128)(2,1)} %param.15) | copy-start | bytes 3538948
  106.1 51.2 %all-to-all-start.3 = ((bf16[128,16,768]{2,1,0:T(8,128)(2,1)}), bf16[128,16,768]{2,1,0:T(8,128)(2,1)}, u32[]{:S(2)}, u32[]{:S(2)}) async-start(bf16[128,16,768]{2,1,0:T(8,128)(2,1)} %broadcast_select_fusion), calls=%async_computation.3 | async-start | bytes 6291456 | tf_op jit(solution)/shard_map/all_to_all | solution.py:161
  119.4 22.1 %copy-start.10 = (f32[768]{0:T(1024)S(1)}, f32[768]{0:T(1024)}, u32[]{:S(2)}) copy-start(f32[768]{0:T(1024)} %param.18) | copy-start | bytes 9220
  157.3 17.3 %all-to-all-start.2 = ((bf16[128,2,896]{2,1,0:T(2,128)(2,1)}), bf16[128,2,896]{2,1,0:T(2,128)(2,1)S(1)}, u32[]{:S(2)}, u32[]{:S(2)}) async-start(bf16[128,2,896]{2,1,0:T(2,128)(2,1)} %all_to_all.28), calls=%async_computation.2 | async-start | bytes 917504 | tf_op jit(solution)/shard_map/all_to_all | solution.py:131
  175.0 2.5 copy-start.5
  177.5 2.2 copy-start.6
  188.8 4.8 %copy-start.11 = (s32[128]{0:T(128)S(1)}, s32[128]{0:T(128)}, u32[]{:S(2)}) copy-start(s32[128]{0:T(128)} %param.23) | copy-start | bytes 1540
  188.8 52.4 %all-to-all-start.4 = ((bf16[128,16,896]{2,1,0:T(8,128)(2,1)}), bf16[128,16,896]{2,1,0:T(8,128)(2,1)}, u32[]{:S(2)}, u32[]{:S(2)}) async-start(bf16[128,16,896]{2,1,0:T(8,128)(2,1)} %copy.109), calls=%async_computation.4 | async-start | bytes 7340032 | tf_op jit(solution)/shard_map/all_to_all | solution.py:176
  248.4 3.8 %copy-start.1 = (bf16[768,768]{1,0:T(8,128)(2,1)S(1)}, bf16[768,768]{1,0:T(8,128)(2,1)}, u32[]{:S(2)}) copy-start(bf16[768,768]{1,0:T(8,128)(2,1)} %param.16) | copy-start | bytes 3538948
Sparse Core Ops, SparseCore 0:
  9.6 55.5 all-gather.1

commit v5 on v4

--- a/solution.py
+++ b/solution.py
@@ -110,24 +110,17 @@
     )
     rank_in = jnp.sum(dest_hits * (jnp.cumsum(dest_hits, axis=0) - 1), axis=1)
     slot_of = dest_of * refresh_cap + rank_in
-    filled = (
-        jnp.full((device_count * refresh_cap,), -1, jnp.int32)
-        .at[slot_of]
-        .set(jnp.arange(docs_here, dtype=jnp.int32))
-    )
-    slot_used = filled >= 0
-    slot_doc = jnp.maximum(filled, 0)
-    code = jnp.where(slot_used, refresh_ids[slot_doc] % rows_own + 1, 0)
+    slot_match = slot_of[:, None] == jnp.arange(device_count * refresh_cap, dtype=jnp.int32)[None, :]
+    code = jnp.sum(
+        jnp.where(slot_match, (refresh_ids % rows_own + 1)[:, None], 0), axis=0
+    )
     code_cols = jnp.zeros((code.shape[0], 128), jnp.float32)
     code_cols = code_cols.at[:, 0].set((code // CODE_BASE).astype(jnp.float32))
     code_cols = code_cols.at[:, 1].set((code % CODE_BASE).astype(jnp.float32))
-    out_rows = jnp.concatenate(
-        [
-            jnp.where(slot_used[:, None], embedded[slot_doc], jnp.zeros((), jnp.bfloat16)),
-            code_cols.astype(jnp.bfloat16),
-        ],
-        axis=1,
-    )
+    slot_rows = jnp.dot(
+        slot_match.T.astype(jnp.bfloat16), embedded, preferred_element_type=jnp.float32
+    ).astype(jnp.bfloat16)
+    out_rows = jnp.concatenate([slot_rows, code_cols.astype(jnp.bfloat16)], axis=1)
     got = lax.all_to_all(out_rows, CACHE + ("mp",), split_axis=0, concat_axis=0, tiled=True)
     got_code = got[:, width].astype(jnp.int32) * CODE_BASE + got[:, width + 1].astype(jnp.int32)
     local_row = got_code - 1

time: 260 us -> 233 us (0.90)
  other arithmetic: 49.4 us -> 30.5 us
  local copies, waits for them, and re-layouts: 54.9 us -> 47.4 us
    another operation x6 -> x5, other arithmetic: 23.2 us -> 5.16 us
    gather x3 -> x0, local copies, waits for them, and re-layouts: 5.08 us -> none  [the longest x2 3.89 us: shards(): code = jnp.where(slot_used, refresh_ids[slot_doc] % rows_own + 1, 0)]
  transfers between devices with their start and end apart: 6 -> 6, of which waited for: 4 -> 4; matrix products, arithmetic and copies ran while one was open for 43% -> 38% of each run, Pallas kernels for 0% -> 0%
where the time goes in v5:
time: 233 us; the launch traced here: 232 us
  waiting for transfers between devices  71.1 us (31%)
  local copies, waits for them, and re-layouts  47.4 us (20%)
  matrix products  36.4 us (16%)
  starting transfers between devices  31.8 us (14%)
  other arithmetic  30.5 us (13%)
  between operations  14.4 us (6%)
    all_to_all x1, waiting for transfers between devices, shards(): lax.all_to_all(packed.reshape(-1, packed.shape[-1]), CACHE + ('mp',), spl...  47.2 us
    dot_general x1, matrix products, shards(): jnp.dot(hidden_rest, w_out_rest, preferred_element_type=jnp.float32)  22.1 us
    all_to_all x1, waiting for transfers between devices, shards(): lax.all_to_all(outbound, CACHE + ('mp',), split_axis=0, concat_axis=0, ti...  10.5 us
    gather x1, local copies, waits for them, and re-layouts, shards(): queries[jnp.maximum(slot_pair, 0) // neg_count]  9.38 us
    all_to_all x1, starting transfers between devices, shards(): lax.all_to_all(outbound, CACHE + ('mp',), split_axis=0, concat_axis=0, ti...  9.19 us
    all_to_all x1, starting transfers between devices, shards(): lax.all_to_all(jnp.broadcast_to(other_pieces[:, None], (mp_count - 1, pie...  9.1 us
    all_to_all x1, waiting for transfers between devices, shards(): lax.all_to_all(out_rows, CACHE + ('mp',), split_axis=0, concat_axis=0, ti...  8.77 us
    dot_general x1, matrix products, shards(): jnp.dot(hidden_own, w_out, preferred_element_type=jnp.float32)  8.58 us
  transfers between devices with their start and end apart: 6, of which 4 were waited for; matrix products, arithmetic and copies ran while one was open for 38% of the time, Pallas kernels for 0%

profile of v5, /device:TPU:1, one launch (start us, length us, event | category | flops | bytes accessed | tf_op | source)
XLA Modules:
  0.0 231.5 jit_solution(18185878521110736862)
XLA Ops:
  9.1 4.8 %all-to-all-start = ((bf16[4,24,768]{2,1,0:T(8,128)(2,1)}), bf16[4,24,768]{2,1,0:T(8,128)(2,1)S(1)}, u32[]{:S(2)}, u32[]{:S(2)}) async-start(bf16[4,24,768]{2,1,0:T(8,128)(2,1)} %broadcast_in_dim.38), calls=%async_computation | async-start | bytes 294912 | tf_op jit(solution)/shard_map/all_to_all | solution.py:65
  16.0 2.7 %fusion.1 = f32[2048]{0:T(1024)S(1)} fusion(bf16[2048,768]{1,0:T(8,128)(2,1)} %param.14), kind=kLoop, calls=%fused_computation.11 | loop fusion | flops 4716544 | bytes 3153920 | tf_op jit(solution)/shard_map/reduce_sum | solution.py:17
  21.2 2.4 %fusion.3 = bf16[2048,768]{1,0:T(8,128)(2,1)} fusion(bf16[2048,768]{1,0:T(8,128)(2,1)S(1)} %copy-done.3, f32[768]{0:T(1024)S(1)} %copy-done.8, f32[2048]{0:T(1024)S(1)} %add_rsqrt_fusion.1), kind=kLoop, calls=%fused_computation.13 | loop fusion | flops 6291456 | bytes 6302720 | tf_op jit(solution)/shard_map/convert_element_type | solution.py:59
  25.9 9.1 %all-to-all-start.1 = ((bf16[3,32,24,768]{3,2,0,1:T(8,128)(2,1)}), bf16[3,32,24,768]{3,2,0,1:T(8,128)(2,1)}, u32[]{:S(2)}, u32[]{:S(2)}) async-start(bf16[3,32,24,768]{3,2,0,1:T(8,128)(2,1)} %broadcast_in_dim.39), calls=%async_computation.1 | async-start | bytes 7077888 | tf_op jit(solution)/shard_map/all_to_all | solution.py:75
  35.8 2.7 %add_add_fusion = s32[1024,8,128]{0,1,2:T(8,128)S(1)} fusion(s32[1024,8,128]{0,1,2:T(8,128)} %fusion.6, s32[1024,8]{0,1:T(8,128)S(1)} %slice.93), kind=kLoop, calls=%fused_computation.21 | loop fusion | flops 2097152 | bytes 8421376 | tf_op jit(solution)/shard_map/sub | solution.py:142
  38.5 4.4 %copy.97 = s32[1024,8,128]{0,2,1:T(8,128)} copy(s32[1024,8,128]{0,1,2:T(8,128)S(1)} %add_add_fusion) | data formatting | bytes 8388608 | tf_op jit(solution)/shard_map/sub | solution.py:142
  43.1 3.0 %fusion.5 = s32[1024]{0:T(1024)S(1)} fusion(s32[1024,8,128]{0,2,1:T(8,128)} %copy.97, s32[1024]{0:T(1024)S(1)} %eq.90), kind=kLoop, calls=%fused_computation.20 | loop fusion | flops 3144704 | bytes 4202496 | tf_op jit(solution)/shard_map/reduce_sum | solution.py:142
  46.2 4.3 %scatter_custom_fusion = s32[2048]{0:T(1024)S(1)} fusion(s32[1024]{0:T(1024)S(1)} %bitcast.86, s32[1024]{0:T(1024)S(1)} %iota.37, s32[]{:T(128)} %constant.171.clone.1), kind=kCustom, calls=%fused_computation.116 | custom fusion | bytes 8196 | tf_op jit(solution)/shard_map/scatter | solution.py:147
  53.6 9.4 %gather_fusion = bf16[2048,768]{1,0:T(8,128)(2,1)} fusion(bf16[128,768]{1,0:T(8,128)(2,1)S(1)} %copy-done.2, s32[2048]{0:T(1024)S(1)} %fusion.43), kind=kCustom, calls=%fused_computation | custom fusion | bytes 6299648 | tf_op jit(solution)/shard_map/gather | solution.py:151
  63.0 3.4 %broadcast_select_fusion = bf16[128,16,768]{2,1,0:T(8,128)(2,1)} fusion(bf16[128,16,768]{2,1,0:T(8,128)(2,1)} %bitcast.81, pred[128,16]{1,0:T(8,128)(4,1)S(1)} %broadcast_in_dim.44), kind=kLoop, calls=%fused_computation.29 | loop fusion | flops 1572864 | bytes 6293504 | tf_op jit(solution)/shard_map/jit(_where)/select_n | solution.py:149
  66.4 8.6 %fusion.19 = f32[2048,768]{1,0:T(8,128)} fusion(bf16[768,768]{1,0:T(8,128)(2,1)S(1)} %copy-done, bf16[2048,768]{1,0:T(8,128)(2,1)} %fusion.3, bf16[768,768]{1,0:T(8,128)(2,1)S(1)} %copy-done.6), kind=kOutput, calls=%fused_computation.43 | convolution fusion | flops 4834983936 | bytes 11796480 | tf_op jit(solution)/shard_map/dot_general | solution.py:97
  75.0 3.9 %all-to-all-done.1 = bf16[3,32,24,768]{3,2,0,1:T(8,128)(2,1)} async-done(((bf16[3,32,24,768]{3,2,0,1:T(8,128)(2,1)}), bf16[3,32,24,768]{3,2,0,1:T(8,128)(2,1)}, u32[]{:S(2)}, u32[]{:S(2)}) %all-to-all-start.1) | async-done | bytes 3538976 | tf_op jit(solution)/shard_map/all_to_all | solution.py:75
  78.9 9.2 %all-to-all-start.3 = ((bf16[128,16,768]{2,1,0:T(8,128)(2,1)}), bf16[128,16,768]{2,1,0:T(8,128)(2,1)}, u32[]{:S(2)}, u32[]{:S(2)}) async-start(bf16[128,16,768]{2,1,0:T(8,128)(2,1)} %broadcast_select_fusion), calls=%async_computation.3 | async-start | bytes 6291456 | tf_op jit(solution)/shard_map/all_to_all | solution.py:154
  88.1 4.0 %copy.88 = bf16[3,32,24,768]{3,2,1,0:T(8,128)(2,1)} copy(bf16[3,32,24,768]{3,2,0,1:T(8,128)(2,1)} %all-to-all-done.1) | data formatting | bytes 7077888 | tf_op jit(solution)/shard_map/all_to_all | solution.py:75
  92.1 22.1 %multiply_reduce_fusion = (f32[2048]{0:T(1024)S(1)}, f32[2048,768]{1,0:T(8,128)}) fusion(f32[2048,768]{1,0:T(8,128)} %fusion.19, bf16[2304,768]{1,0:T(8,128)(2,1)} %bitcast.84, bf16[2048,768]{1,0:T(8,128)(2,1)} %fusion.3, s32[]{:T(128)S(6)} %select_n.76, bf16[768,3072]{1,0:T(8,128)(2,1)} %all-gather.2.cloned.1.call-done, bf16[2048,768]{1,0:T(8,128)(2,1)} %param.14), kind=kOutput, calls=%fused_computation.16 | convolution fusion | flops 14519891968 | bytes 27140100 | tf_op jit(solution)/shard_map/dot_general | solution.py:97
  114.2 3.8 %bitcast_reduce_fusion = f32[32,768]{1,0:T(8,128)S(1)} fusion(f32[2048,768]{1,0:T(8,128)} %get-tuple-element.43, f32[768]{0:T(1024)S(1)} %copy-done.9, f32[2048]{0:T(1024)S(1)} %add_rsqrt_fusion), kind=kLoop, calls=%fused_computation.14 | loop fusion | flops 4694016 | bytes 6401024 | tf_op jit(solution)/shard_map/reduce_sum | solution.py:102
  119.6 10.5 %all-to-all-done.3 = bf16[128,16,768]{2,1,0:T(8,128)(2,1)} async-done(((bf16[128,16,768]{2,1,0:T(8,128)(2,1)}), bf16[128,16,768]{2,1,0:T(8,128)(2,1)}, u32[]{:S(2)}, u32[]{:S(2)}) %all-to-all-start.3) | async-done | bytes 3145760 | tf_op jit(solution)/shard_map/all_to_all | solution.py:154
  130.0 3.8 %all-to-all-start.2 = ((bf16[128,2,896]{2,1,0:T(2,128)(2,1)}), bf16[128,2,896]{2,1,0:T(2,128)(2,1)S(1)}, u32[]{:S(2)}, u32[]{:S(2)}) async-start(bf16[128,2,896]{2,1,0:T(2,128)(2,1)} %all_to_all.28), calls=%async_computation.2 | async-start | bytes 917504 | tf_op jit(solution)/shard_map/all_to_all | solution.py:124
  133.8 4.6 %copy.98 = bf16[128,16,768]{2,0,1:T(8,128)(2,1)} copy(bf16[128,16,768]{2,1,0:T(8,128)(2,1)} %all-to-all-done.3) | data formatting | bytes 6291456 | tf_op jit(solution)/shard_map/all_to_all | solution.py:154
  138.4 8.8 %all-to-all-done.2 = bf16[128,2,896]{2,1,0:T(2,128)(2,1)S(1)} async-done(((bf16[128,2,896]{2,1,0:T(2,128)(2,1)}), bf16[128,2,896]{2,1,0:T(2,128)(2,1)S(1)}, u32[]{:S(2)}, u32[]{:S(2)}) %all-to-all-start.2) | async-done | bytes 458784 | tf_op jit(solution)/shard_map/all_to_all | solution.py:124
  154.8 6.5 %copy.104 = bf16[128,16,896]{2,1,0:T(8,128)(2,1)} copy(bf16[128,16,896]{0,2,1:T(8,128)(2,1)} %bitcast.79) | data formatting | bytes 7340032 | tf_op jit(solution)/shard_map/all_to_all | solution.py:169
  161.3 4.8 %all-to-all-start.4 = ((bf16[128,16,896]{2,1,0:T(8,128)(2,1)}), bf16[128,16,896]{2,1,0:T(8,128)(2,1)}, u32[]{:S(2)}, u32[]{:S(2)}) async-start(bf16[128,16,896]{2,1,0:T(8,128)(2,1)} %copy.104), calls=%async_computation.4 | async-start | bytes 7340032 | tf_op jit(solution)/shard_map/all_to_all | solution.py:169
  166.5 47.2 %all-to-all-done.4 = bf16[128,16,896]{2,1,0:T(8,128)(2,1)} async-done(((bf16[128,16,896]{2,1,0:T(8,128)(2,1)}), bf16[128,16,896]{2,1,0:T(8,128)(2,1)}, u32[]{:S(2)}, u32[]{:S(2)}) %all-to-all-start.4) | async-done | bytes 3670048 | tf_op jit(solution)/shard_map/all_to_all | solution.py:169
  213.7 7.2 %gather_fusion.1 = bf16[1024,896]{1,0:T(8,128)(2,1)S(1)} fusion(bf16[2048,896]{1,0:T(8,128)(2,1)} %bitcast.19, s32[1024]{0:T(1024)S(1)} %broadcast_clamp_fusion), kind=kCustom, calls=%fused_computation.1 | custom fusion | bytes 3674112 | tf_op jit(solution)/shard_map/gather | solution.py:172
  (92 shorter events, 25.9 us)
Async XLA Ops:
  7.2 1.3 copy-start
  7.2 84.9 %all-gather.2.cloned.1.call-start = ((), (), s32[]{:S(2)}) async-start(), calls=%async_computation.5 | async-start | bytes 5898240 | tf_op jit(solution)/shard_map/all_gather | solution.py:83
  9.1 14.7 %all-to-all-start = ((bf16[4,24,768]{2,1,0:T(8,128)(2,1)}), bf16[4,24,768]{2,1,0:T(8,128)(2,1)S(1)}, u32[]{:S(2)}, u32[]{:S(2)}) async-start(bf16[4,24,768]{2,1,0:T(8,128)(2,1)} %broadcast_in_dim.38), calls=%async_computation | async-start | bytes 294912 | tf_op jit(solution)/shard_map/all_to_all | solution.py:65
  16.0 5.2 %copy-start.3 = (bf16[2048,768]{1,0:T(8,128)(2,1)S(1)}, bf16[2048,768]{1,0:T(8,128)(2,1)}, u32[]{:S(2)}) copy-start(bf16[2048,768]{1,0:T(8,128)(2,1)} %param.14) | copy-start | bytes 9437188
  16.0 5.2 %copy-start.8 = (f32[768]{0:T(1024)S(1)}, f32[768]{0:T(1024)}, u32[]{:S(2)}) copy-start(f32[768]{0:T(1024)} %param.17) | copy-start | bytes 9220
  25.9 53.0 %all-to-all-start.1 = ((bf16[3,32,24,768]{3,2,0,1:T(8,128)(2,1)}), bf16[3,32,24,768]{3,2,0,1:T(8,128)(2,1)}, u32[]{:S(2)}, u32[]{:S(2)}) async-start(bf16[3,32,24,768]{3,2,0,1:T(8,128)(2,1)} %broadcast_in_dim.39), calls=%async_computation.1 | async-start | bytes 7077888 | tf_op jit(solution)/shard_map/all_to_all | solution.py:75
  38.5 4.4 %copy-start.7 = (s32[128,8]{0,1:T(8,128)S(1)}, s32[128,8]{0,1:T(8,128)}, u32[]{:S(2)}) copy-start(s32[128,8]{0,1:T(8,128)} %param.22) | copy-start | bytes 12292
  42.9 10.7 %copy-start.2 = (bf16[128,768]{1,0:T(8,128)(2,1)S(1)}, bf16[128,768]{1,0:T(8,128)(2,1)}, u32[]{:S(2)}) copy-start(bf16[128,768]{1,0:T(8,128)(2,1)} %param.21) | copy-start | bytes 589828
  63.0 3.4 %copy-start.6 = (bf16[768,768]{1,0:T(8,128)(2,1)S(1)}, bf16[768,768]{1,0:T(8,128)(2,1)}, u32[]{:S(2)}) copy-start(bf16[768,768]{1,0:T(8,128)(2,1)} %param.15) | copy-start | bytes 3538948
  78.9 51.1 %all-to-all-start.3 = ((bf16[128,16,768]{2,1,0:T(8,128)(2,1)}), bf16[128,16,768]{2,1,0:T(8,128)(2,1)}, u32[]{:S(2)}, u32[]{:S(2)}) async-start(bf16[128,16,768]{2,1,0:T(8,128)(2,1)} %broadcast_select_fusion), calls=%async_computation.3 | async-start | bytes 6291456 | tf_op jit(solution)/shard_map/all_to_all | solution.py:154
  92.1 22.1 %copy-start.9 = (f32[768]{0:T(1024)S(1)}, f32[768]{0:T(1024)}, u32[]{:S(2)}) copy-start(f32[768]{0:T(1024)} %param.18) | copy-start | bytes 9220
  130.0 17.1 %all-to-all-start.2 = ((bf16[128,2,896]{2,1,0:T(2,128)(2,1)}), bf16[128,2,896]{2,1,0:T(2,128)(2,1)S(1)}, u32[]{:S(2)}, u32[]{:S(2)}) async-start(bf16[128,2,896]{2,1,0:T(2,128)(2,1)} %all_to_all.28), calls=%async_computation.2 | async-start | bytes 917504 | tf_op jit(solution)/shard_map/all_to_all | solution.py:124
  147.3 2.7 %copy-start.4 = (bf16[128,16,768]{2,0,1:T(8,128)(2,1)S(1)}, bf16[128,16,768]{2,0,1:T(8,128)(2,1)}, u32[]{:S(2)}) copy-start(bf16[128,16,768]{2,0,1:T(8,128)(2,1)} %copy.98) | copy-start | bytes 9437188
  150.0 2.2 copy-start.5
  161.3 4.8 %copy-start.10 = (s32[128]{0:T(128)S(1)}, s32[128]{0:T(128)}, u32[]{:S(2)}) copy-start(s32[128]{0:T(128)} %param.23) | copy-start | bytes 1540
  161.3 52.4 %all-to-all-start.4 = ((bf16[128,16,896]{2,1,0:T(8,128)(2,1)}), bf16[128,16,896]{2,1,0:T(8,128)(2,1)}, u32[]{:S(2)}, u32[]{:S(2)}) async-start(bf16[128,16,896]{2,1,0:T(8,128)(2,1)} %copy.104), calls=%async_computation.4 | async-start | bytes 7340032 | tf_op jit(solution)/shard_map/all_to_all | solution.py:169
  220.9 3.8 %copy-start.1 = (bf16[768,768]{1,0:T(8,128)(2,1)S(1)}, bf16[768,768]{1,0:T(8,128)(2,1)}, u32[]{:S(2)}) copy-start(bf16[768,768]{1,0:T(8,128)(2,1)} %param.16) | copy-start | bytes 3538948
Sparse Core Ops, SparseCore 0:
  9.6 55.5 all-gather.1

commit v6 on v5

--- a/solution.py
+++ b/solution.py
@@ -141,16 +141,11 @@
     )
     pair_rank = jnp.sum(pair_marks * (jnp.cumsum(pair_marks, axis=0) - 1), axis=1)
     pair_slots = pair_blocks * query_cap + pair_rank
-    slot_pair = (
-        jnp.full((block_count * query_cap,), -1, jnp.int32)
-        .at[pair_slots]
-        .set(jnp.arange(pair_count, dtype=jnp.int32))
-    )
-    outbound = jnp.where(
-        (slot_pair >= 0)[:, None],
-        queries[jnp.maximum(slot_pair, 0) // neg_count],
-        jnp.zeros((), jnp.bfloat16),
-    )
+    pair_match = pair_slots[:, None] == jnp.arange(block_count * query_cap, dtype=jnp.int32)[None, :]
+    slot_query = jnp.any(pair_match.reshape(query_count, neg_count, -1), axis=1)
+    outbound = jnp.dot(
+        slot_query.T.astype(jnp.bfloat16), queries, preferred_element_type=jnp.float32
+    ).astype(jnp.bfloat16)
     arrived = lax.all_to_all(outbound, CACHE + ("mp",), split_axis=0, concat_axis=0, tiled=True)
     arrived = arrived.reshape(device_count, local_blocks, query_cap, width)
     block_keys = fresh_cache.reshape(local_blocks, BLOCK, width)
@@ -169,7 +164,9 @@
     back = lax.all_to_all(
         packed.reshape(-1, packed.shape[-1]), CACHE + ("mp",), split_axis=0, concat_axis=0, tiled=True
     )
-    pair_back = back[pair_slots].astype(jnp.float32)
+    pair_back = jnp.dot(
+        pair_match.astype(jnp.bfloat16), back, preferred_element_type=jnp.float32
+    )
     pair_mix = pair_back[:, :width].reshape(query_count, neg_count, width)
     pair_peak = join_parts(pair_back[:, width : width + 3]).reshape(query_count, neg_count)
     pair_total = join_parts(pair_back[:, width + 3 : width + 6]).reshape(query_count, neg_count)

time: 233 us -> 230 us (0.987)
  local copies, waits for them, and re-layouts: 47.4 us -> 27 us
  waiting for transfers between devices: 71.1 us -> 83.2 us
  matrix products: 36.4 us -> 47 us
  other arithmetic: 30.5 us -> 25.6 us
    gather x2 -> x0, local copies, waits for them, and re-layouts: 16.5 us -> none  [the longest x1 9.38 us: shards(): queries[jnp.maximum(slot_pair, 0) // neg_count]]
    all_to_all x1, waiting for transfers between devices: 3.93 us -> 16.1 us  [shards(): lax.all_to_all(jnp.broadcast_to(other_pieces[:, None], (mp_count - 1, pie...]
    dot_general x0 -> x2, matrix products: none -> 9.21 us  [the longest x1 6.49 us: shards(): jnp.dot(pair_match.astype(jnp.bfloat16), back, preferred_element_type=jnp...]
    scatter x1 -> x0, local copies, waits for them, and re-layouts: 4.32 us -> none  [shards(): slot_pair = jnp.full((block_count * query_cap,), -1, jnp.int32).at[pair_s...]
    reduce_or x0 -> x1, other arithmetic: none -> 3.97 us  [shards(): slot_query = jnp.any(pair_match.reshape(query_count, neg_count, -1), axis=1)]
    select_n x2 -> x0, other arithmetic: 3.41 us -> none  [the longest x1 3.4 us: shards(): jnp.where((slot_pair >= 0)[:, None], queries[jnp.maximum(slot_pair, 0) //...]
  transfers between devices with their start and end apart: 6 -> 6, of which waited for: 4 -> 4; matrix products, arithmetic and copies ran while one was open for 38% -> 31% of each run, Pallas kernels for 0% -> 0%
where the time goes in v6:
time: 230 us; the launch traced here: 229 us
  waiting for transfers between devices  83.2 us (36%)
  matrix products  47 us (20%)
  starting transfers between devices  31.9 us (14%)
  local copies, waits for them, and re-layouts  27 us (12%)
  other arithmetic  25.6 us (11%)
  between operations  14.4 us (6%)
    all_to_all x1, waiting for transfers between devices, shards(): lax.all_to_all(packed.reshape(-1, packed.shape[-1]), CACHE + ('mp',), spl...  47.2 us
    dot_general x1, matrix products, shards(): jnp.dot(hidden_rest, w_out_rest, preferred_element_type=jnp.float32)  22.1 us
    all_to_all x1, waiting for transfers between devices, shards(): lax.all_to_all(jnp.broadcast_to(other_pieces[:, None], (mp_count - 1, pie...  16.1 us
    all_to_all x1, waiting for transfers between devices, shards(): lax.all_to_all(outbound, CACHE + ('mp',), split_axis=0, concat_axis=0, ti...  10.5 us
    all_to_all x1, starting transfers between devices, shards(): lax.all_to_all(jnp.broadcast_to(other_pieces[:, None], (mp_count - 1, pie...  9.23 us
    all_to_all x1, starting transfers between devices, shards(): lax.all_to_all(outbound, CACHE + ('mp',), split_axis=0, concat_axis=0, ti...  9.2 us
    all_to_all x1, waiting for transfers between devices, shards(): lax.all_to_all(out_rows, CACHE + ('mp',), split_axis=0, concat_axis=0, ti...  8.73 us
    dot_general x1, matrix products, shards(): jnp.dot(hidden_own, w_out, preferred_element_type=jnp.float32)  8.61 us
  transfers between devices with their start and end apart: 6, of which 4 were waited for; matrix products, arithmetic and copies ran while one was open for 31% of the time, Pallas kernels for 0%

profile of v6, /device:TPU:1, one launch (start us, length us, event | category | flops | bytes accessed | tf_op | source)
XLA Modules:
  0.0 229.2 jit_solution(17878596180561697477)
XLA Ops:
  9.1 4.8 %all-to-all-start = ((bf16[4,24,768]{2,1,0:T(8,128)(2,1)}), bf16[4,24,768]{2,1,0:T(8,128)(2,1)S(1)}, u32[]{:S(2)}, u32[]{:S(2)}) async-start(bf16[4,24,768]{2,1,0:T(8,128)(2,1)} %broadcast_in_dim.17), calls=%async_computation | async-start | bytes 294912 | tf_op jit(solution)/shard_map/all_to_all | solution.py:65
  14.9 2.7 %fusion.3 = f32[2048]{0:T(1024)S(1)} fusion(bf16[2048,768]{1,0:T(8,128)(2,1)} %param.14), kind=kLoop, calls=%fused_computation.12 | loop fusion | flops 4716544 | bytes 3153920 | tf_op jit(solution)/shard_map/reduce_sum | solution.py:17
  17.7 2.4 %fusion.5 = bf16[2048,768]{1,0:T(8,128)(2,1)} fusion(bf16[2048,768]{1,0:T(8,128)(2,1)S(1)} %copy-done.3, f32[768]{0:T(1024)S(1)} %copy-done.9, f32[2048]{0:T(1024)S(1)} %add_rsqrt_fusion.1), kind=kLoop, calls=%fused_computation.14 | loop fusion | flops 6291456 | bytes 6302720 | tf_op jit(solution)/shard_map/convert_element_type | solution.py:59
  22.2 9.2 %all-to-all-start.1 = ((bf16[3,32,24,768]{3,2,0,1:T(8,128)(2,1)}), bf16[3,32,24,768]{3,2,0,1:T(8,128)(2,1)}, u32[]{:S(2)}, u32[]{:S(2)}) async-start(bf16[3,32,24,768]{3,2,0,1:T(8,128)(2,1)} %broadcast_in_dim.18), calls=%async_computation.1 | async-start | bytes 7077888 | tf_op jit(solution)/shard_map/all_to_all | solution.py:75
  34.5 2.7 %add_add_fusion = s32[1024,8,128]{0,1,2:T(8,128)S(1)} fusion(s32[1024,8,128]{0,1,2:T(8,128)} %copy-done.2, s32[1024,8]{0,1:T(8,128)S(1)} %slice.89), kind=kLoop, calls=%fused_computation.23 | loop fusion | flops 2097152 | bytes 8421376 | tf_op jit(solution)/shard_map/sub | solution.py:142
  37.2 2.4 %copy.105 = s32[1024,8,128]{0,2,1:T(8,128)S(1)} copy(s32[1024,8,128]{0,1,2:T(8,128)S(1)} %add_add_fusion) | data formatting | bytes 8388608 | tf_op jit(solution)/shard_map/sub | solution.py:142
  43.9 4.0 %fusion.1 = pred[128,2048]{1,0:T(8,128)(4,1)S(1)} fusion(s32[128,8]{1,0:T(8,128)S(1)} %copy.107), kind=kLoop, calls=%fused_computation.9 | loop fusion | flops 3932160 | bytes 266240 | tf_op jit(solution)/shard_map/reduce_or | solution.py:145
  47.9 2.7 %convolution_convert_fusion = bf16[2048,768]{1,0:T(8,128)(2,1)} fusion(pred[128,2048]{1,0:T(8,128)(4,1)S(1)} %fusion.1, bf16[128,768]{1,0:T(8,128)(2,1)S(1)} %copy-done.7), kind=kOutput, calls=%fused_computation.30 | convolution fusion | flops 404226048 | bytes 3604480 | tf_op jit(solution)/shard_map/dot_general | solution.py:146
  50.6 8.6 %fusion.23 = f32[2048,768]{1,0:T(8,128)} fusion(bf16[768,768]{1,0:T(8,128)(2,1)S(1)} %copy-done, bf16[2048,768]{1,0:T(8,128)(2,1)} %fusion.5, bf16[768,768]{1,0:T(8,128)(2,1)S(1)} %copy-done.6), kind=kOutput, calls=%fused_computation.45 | convolution fusion | flops 4834983936 | bytes 11796480 | tf_op jit(solution)/shard_map/dot_general | solution.py:97
  59.2 16.1 %all-to-all-done.1 = bf16[3,32,24,768]{3,2,0,1:T(8,128)(2,1)} async-done(((bf16[3,32,24,768]{3,2,0,1:T(8,128)(2,1)}), bf16[3,32,24,768]{3,2,0,1:T(8,128)(2,1)}, u32[]{:S(2)}, u32[]{:S(2)}) %all-to-all-start.1) | async-done | bytes 3538976 | tf_op jit(solution)/shard_map/all_to_all | solution.py:75
  75.3 9.2 %all-to-all-start.3 = ((bf16[128,16,768]{2,1,0:T(8,128)(2,1)}), bf16[128,16,768]{2,1,0:T(8,128)(2,1)}, u32[]{:S(2)}, u32[]{:S(2)}) async-start(bf16[128,16,768]{2,1,0:T(8,128)(2,1)} %bitcast.81), calls=%async_computation.3 | async-start | bytes 6291456 | tf_op jit(solution)/shard_map/all_to_all | solution.py:149
  84.5 4.0 %copy.97 = bf16[3,32,24,768]{3,2,1,0:T(8,128)(2,1)} copy(bf16[3,32,24,768]{3,2,0,1:T(8,128)(2,1)} %all-to-all-done.1) | data formatting | bytes 7077888 | tf_op jit(solution)/shard_map/all_to_all | solution.py:75
  88.5 22.1 %multiply_reduce_fusion = (f32[2048]{0:T(1024)S(1)}, f32[2048,768]{1,0:T(8,128)}) fusion(f32[2048,768]{1,0:T(8,128)} %fusion.23, bf16[2304,768]{1,0:T(8,128)(2,1)} %bitcast.85, bf16[2048,768]{1,0:T(8,128)(2,1)} %fusion.5, s32[]{:T(128)S(6)} %select_n.52, bf16[768,3072]{1,0:T(8,128)(2,1)} %all-gather.2.cloned.1.call-done, bf16[2048,768]{1,0:T(8,128)(2,1)} %param.14), kind=kOutput, calls=%fused_computation.17 | convolution fusion | flops 14519891968 | bytes 27140100 | tf_op jit(solution)/shard_map/dot_general | solution.py:97
  110.7 3.8 %bitcast_reduce_fusion = f32[32,768]{1,0:T(8,128)S(1)} fusion(f32[2048,768]{1,0:T(8,128)} %get-tuple-element.43, f32[768]{0:T(1024)S(1)} %copy-done.10, f32[2048]{0:T(1024)S(1)} %add_rsqrt_fusion), kind=kLoop, calls=%fused_computation.15 | loop fusion | flops 4694016 | bytes 6401024 | tf_op jit(solution)/shard_map/reduce_sum | solution.py:102
  116.0 10.5 %all-to-all-done.3 = bf16[128,16,768]{2,1,0:T(8,128)(2,1)} async-done(((bf16[128,16,768]{2,1,0:T(8,128)(2,1)}), bf16[128,16,768]{2,1,0:T(8,128)(2,1)}, u32[]{:S(2)}, u32[]{:S(2)}) %all-to-all-start.3) | async-done | bytes 3145760 | tf_op jit(solution)/shard_map/all_to_all | solution.py:149
  126.4 3.8 %all-to-all-start.2 = ((bf16[128,2,896]{2,1,0:T(2,128)(2,1)}), bf16[128,2,896]{2,1,0:T(2,128)(2,1)S(1)}, u32[]{:S(2)}, u32[]{:S(2)}) async-start(bf16[128,2,896]{2,1,0:T(2,128)(2,1)} %all_to_all.30), calls=%async_computation.2 | async-start | bytes 917504 | tf_op jit(solution)/shard_map/all_to_all | solution.py:124
  130.2 4.6 %copy.108 = bf16[128,16,768]{2,0,1:T(8,128)(2,1)} copy(bf16[128,16,768]{2,1,0:T(8,128)(2,1)} %all-to-all-done.3) | data formatting | bytes 6291456 | tf_op jit(solution)/shard_map/all_to_all | solution.py:149
  134.8 8.7 %all-to-all-done.2 = bf16[128,2,896]{2,1,0:T(2,128)(2,1)S(1)} async-done(((bf16[128,2,896]{2,1,0:T(2,128)(2,1)}), bf16[128,2,896]{2,1,0:T(2,128)(2,1)S(1)}, u32[]{:S(2)}, u32[]{:S(2)}) %all-to-all-start.2) | async-done | bytes 458784 | tf_op jit(solution)/shard_map/all_to_all | solution.py:124
  144.1 2.2 broadcast_select_fusion
  148.9 2.3 fusion.11
  151.1 6.5 %copy.114 = bf16[128,16,896]{2,1,0:T(8,128)(2,1)} copy(bf16[128,16,896]{0,2,1:T(8,128)(2,1)} %bitcast.80) | data formatting | bytes 7340032 | tf_op jit(solution)/shard_map/all_to_all | solution.py:164
  157.7 4.8 %all-to-all-start.4 = ((bf16[128,16,896]{2,1,0:T(8,128)(2,1)}), bf16[128,16,896]{2,1,0:T(8,128)(2,1)}, u32[]{:S(2)}, u32[]{:S(2)}) async-start(bf16[128,16,896]{2,1,0:T(8,128)(2,1)} %copy.114), calls=%async_computation.4 | async-start | bytes 7340032 | tf_op jit(solution)/shard_map/all_to_all | solution.py:164
  162.9 47.2 %all-to-all-done.4 = bf16[128,16,896]{2,1,0:T(8,128)(2,1)} async-done(((bf16[128,16,896]{2,1,0:T(8,128)(2,1)}), bf16[128,16,896]{2,1,0:T(8,128)(2,1)}, u32[]{:S(2)}, u32[]{:S(2)}) %all-to-all-start.4) | async-done | bytes 3670048 | tf_op jit(solution)/shard_map/all_to_all | solution.py:164
  210.1 6.5 %fusion = f32[1024,896]{0,1:T(8,128)S(1)} fusion(bf16[2048,896]{1,0:T(8,128)(2,1)} %bitcast.17, s32[1024]{0:T(1024)S(1)} %multiply_add_fusion.1), kind=kOutput, calls=%fused_computation.8 | convolution fusion | flops 3760193536 | bytes 7344128 | tf_op jit(solution)/shard_map/dot_general | solution.py:167
  (90 shorter events, 22.8 us)
Async XLA Ops:
  7.2 1.3 copy-start
  7.2 10.5 %copy-start.9 = (f32[768]{0:T(1024)S(1)}, f32[768]{0:T(1024)}, u32[]{:S(2)}) copy-start(f32[768]{0:T(1024)} %param.17) | copy-start | bytes 9220
  7.2 81.3 %all-gather.2.cloned.1.call-start = ((), (), s32[]{:S(2)}) async-start(), calls=%async_computation.5 | async-start | bytes 5898240 | tf_op jit(solution)/shard_map/all_gather | solution.py:83
  9.1 11.0 %all-to-all-start = ((bf16[4,24,768]{2,1,0:T(8,128)(2,1)}), bf16[4,24,768]{2,1,0:T(8,128)(2,1)S(1)}, u32[]{:S(2)}, u32[]{:S(2)}) async-start(bf16[4,24,768]{2,1,0:T(8,128)(2,1)} %broadcast_in_dim.17), calls=%async_computation | async-start | bytes 294912 | tf_op jit(solution)/shard_map/all_to_all | solution.py:65
  14.7 2.9 %copy-start.3 = (bf16[2048,768]{1,0:T(8,128)(2,1)S(1)}, bf16[2048,768]{1,0:T(8,128)(2,1)}, u32[]{:S(2)}) copy-start(bf16[2048,768]{1,0:T(8,128)(2,1)} %param.14) | copy-start | bytes 9437188
  22.2 9.3 %copy-start.8 = (s32[128,8]{0,1:T(8,128)S(1)}, s32[128,8]{0,1:T(8,128)}, u32[]{:S(2)}) copy-start(s32[128,8]{0,1:T(8,128)} %param.22) | copy-start | bytes 12292
  22.2 53.2 %all-to-all-start.1 = ((bf16[3,32,24,768]{3,2,0,1:T(8,128)(2,1)}), bf16[3,32,24,768]{3,2,0,1:T(8,128)(2,1)}, u32[]{:S(2)}, u32[]{:S(2)}) async-start(bf16[3,32,24,768]{3,2,0,1:T(8,128)(2,1)} %broadcast_in_dim.18), calls=%async_computation.1 | async-start | bytes 7077888 | tf_op jit(solution)/shard_map/all_to_all | solution.py:75
  32.5 1.9 copy-start.2
  39.7 8.2 %copy-start.7 = (bf16[128,768]{1,0:T(8,128)(2,1)S(1)}, bf16[128,768]{1,0:T(8,128)(2,1)}, u32[]{:S(2)}) copy-start(bf16[128,768]{1,0:T(8,128)(2,1)} %param.21) | copy-start | bytes 589828
  39.7 10.9 %copy-start.6 = (bf16[768,768]{1,0:T(8,128)(2,1)S(1)}, bf16[768,768]{1,0:T(8,128)(2,1)}, u32[]{:S(2)}) copy-start(bf16[768,768]{1,0:T(8,128)(2,1)} %param.15) | copy-start | bytes 3538948
  75.3 51.1 %all-to-all-start.3 = ((bf16[128,16,768]{2,1,0:T(8,128)(2,1)}), bf16[128,16,768]{2,1,0:T(8,128)(2,1)}, u32[]{:S(2)}, u32[]{:S(2)}) async-start(bf16[128,16,768]{2,1,0:T(8,128)(2,1)} %bitcast.81), calls=%async_computation.3 | async-start | bytes 6291456 | tf_op jit(solution)/shard_map/all_to_all | solution.py:149
  88.5 22.1 %copy-start.10 = (f32[768]{0:T(1024)S(1)}, f32[768]{0:T(1024)}, u32[]{:S(2)}) copy-start(f32[768]{0:T(1024)} %param.18) | copy-start | bytes 9220
  126.4 17.1 %all-to-all-start.2 = ((bf16[128,2,896]{2,1,0:T(2,128)(2,1)}), bf16[128,2,896]{2,1,0:T(2,128)(2,1)S(1)}, u32[]{:S(2)}, u32[]{:S(2)}) async-start(bf16[128,2,896]{2,1,0:T(2,128)(2,1)} %all_to_all.30), calls=%async_computation.2 | async-start | bytes 917504 | tf_op jit(solution)/shard_map/all_to_all | solution.py:124
  143.7 2.7 %copy-start.4 = (bf16[128,16,768]{2,0,1:T(8,128)(2,1)S(1)}, bf16[128,16,768]{2,0,1:T(8,128)(2,1)}, u32[]{:S(2)}) copy-start(bf16[128,16,768]{2,0,1:T(8,128)(2,1)} %copy.108) | copy-start | bytes 9437188
  146.4 2.2 copy-start.5
  157.7 4.8 %copy-start.11 = (s32[128]{0:T(128)S(1)}, s32[128]{0:T(128)}, u32[]{:S(2)}) copy-start(s32[128]{0:T(128)} %param.23) | copy-start | bytes 1540
  157.7 52.4 %all-to-all-start.4 = ((bf16[128,16,896]{2,1,0:T(8,128)(2,1)}), bf16[128,16,896]{2,1,0:T(8,128)(2,1)}, u32[]{:S(2)}, u32[]{:S(2)}) async-start(bf16[128,16,896]{2,1,0:T(8,128)(2,1)} %copy.114), calls=%async_computation.4 | async-start | bytes 7340032 | tf_op jit(solution)/shard_map/all_to_all | solution.py:164
  216.6 5.8 %copy-start.1 = (bf16[768,768]{1,0:T(8,128)(2,1)S(1)}, bf16[768,768]{1,0:T(8,128)(2,1)}, u32[]{:S(2)}) copy-start(bf16[768,768]{1,0:T(8,128)(2,1)} %param.16) | copy-start | bytes 3538948
Sparse Core Ops, SparseCore 0:
  9.7 55.5 all-gather.1

commit v7 on v6

--- a/solution.py
+++ b/solution.py
@@ -165,11 +165,10 @@
         packed.reshape(-1, packed.shape[-1]), CACHE + ("mp",), split_axis=0, concat_axis=0, tiled=True
     )
     pair_back = jnp.dot(
-        pair_match.astype(jnp.bfloat16), back, preferred_element_type=jnp.float32
-    )
-    pair_mix = pair_back[:, :width].reshape(query_count, neg_count, width)
-    pair_peak = join_parts(pair_back[:, width : width + 3]).reshape(query_count, neg_count)
-    pair_total = join_parts(pair_back[:, width + 3 : width + 6]).reshape(query_count, neg_count)
+        pair_match.astype(jnp.bfloat16), back[:, width:], preferred_element_type=jnp.float32
+    )
+    pair_peak = join_parts(pair_back[:, 0:3]).reshape(query_count, neg_count)
+    pair_total = join_parts(pair_back[:, 3:6]).reshape(query_count, neg_count)
     pick_table = (positive_ids[:, None] == jnp.arange(docs_here, dtype=jnp.int32)[None, :]).astype(
         jnp.bfloat16
     )
@@ -183,8 +182,20 @@
     positive_weight = jnp.exp(positive_logit - top_value)
     partition = jnp.sum(block_weight * pair_total, axis=-1) + positive_weight
     loss = top_value + jnp.log(partition) - positive_logit
+    slot_weight = jnp.sum(
+        jnp.where(
+            pair_match.reshape(query_count, neg_count, -1), block_weight[:, :, None], 0.0
+        ),
+        axis=1,
+    )
     pulled = (
-        jnp.einsum("qn,qnd->qd", block_weight, pair_mix) + positive_weight[:, None] * positive_f
+        jnp.dot(
+            slot_weight,
+            back[:, :width].astype(jnp.float32),
+            precision=lax.Precision.HIGHEST,
+            preferred_element_type=jnp.float32,
+        )
+        + positive_weight[:, None] * positive_f
     )
     query_grad = logit_scale * (pulled / partition[:, None] - positive_f)
     return (fresh_cache, loss, query_grad)

time: 230 us -> 229 us (level)
    reduce_sum x0 -> x1, other arithmetic: none -> 2.76 us  [shards(): jnp.sum(jnp.where(pair_match.reshape(query_count, neg_count, -1), block_w...]
where the time goes in v7:
time: 229 us; the launch traced here: 228 us
  waiting for transfers between devices  83.2 us (36%)
  matrix products  45.6 us (20%)
  starting transfers between devices  31.9 us (14%)
  other arithmetic  27.5 us (12%)
  local copies, waits for them, and re-layouts  25.2 us (11%)
  between operations  14.4 us (6%)
    all_to_all x1, waiting for transfers between devices, shards(): lax.all_to_all(packed.reshape(-1, packed.shape[-1]), CACHE + ('mp',), spl...  47.2 us
    dot_general x1, matrix products, shards(): jnp.dot(hidden_rest, w_out_rest, preferred_element_type=jnp.float32)  22.1 us
    all_to_all x1, waiting for transfers between devices, shards(): lax.all_to_all(jnp.broadcast_to(other_pieces[:, None], (mp_count - 1, pie...  16.1 us
    all_to_all x1, waiting for transfers between devices, shards(): lax.all_to_all(outbound, CACHE + ('mp',), split_axis=0, concat_axis=0, ti...  10.5 us
    all_to_all x1, starting transfers between devices, shards(): lax.all_to_all(jnp.broadcast_to(other_pieces[:, None], (mp_count - 1, pie...  9.23 us
    all_to_all x1, starting transfers between devices, shards(): lax.all_to_all(outbound, CACHE + ('mp',), split_axis=0, concat_axis=0, ti...  9.2 us
    all_to_all x1, waiting for transfers between devices, shards(): lax.all_to_all(out_rows, CACHE + ('mp',), split_axis=0, concat_axis=0, ti...  8.73 us
    dot_general x1, matrix products, shards(): jnp.dot(hidden_own, w_out, preferred_element_type=jnp.float32)  8.61 us
  transfers between devices with their start and end apart: 6, of which 4 were waited for; matrix products, arithmetic and copies ran while one was open for 31% of the time, Pallas kernels for 0%

profile of v7, /device:TPU:1, one launch (start us, length us, event | category | flops | bytes accessed | tf_op | source)
XLA Modules:
  0.0 227.8 jit_solution(4171746978073724966)
XLA Ops:
  9.1 4.8 %all-to-all-start = ((bf16[4,24,768]{2,1,0:T(8,128)(2,1)}), bf16[4,24,768]{2,1,0:T(8,128)(2,1)S(1)}, u32[]{:S(2)}, u32[]{:S(2)}) async-start(bf16[4,24,768]{2,1,0:T(8,128)(2,1)} %broadcast_in_dim.29), calls=%async_computation | async-start | bytes 294912 | tf_op jit(solution)/shard_map/all_to_all | solution.py:65
  14.9 2.7 %fusion.3 = f32[2048]{0:T(1024)S(1)} fusion(bf16[2048,768]{1,0:T(8,128)(2,1)} %param.14), kind=kLoop, calls=%fused_computation.13 | loop fusion | flops 4716544 | bytes 3153920 | tf_op jit(solution)/shard_map/reduce_sum | solution.py:17
  17.7 2.4 %fusion.5 = bf16[2048,768]{1,0:T(8,128)(2,1)} fusion(bf16[2048,768]{1,0:T(8,128)(2,1)S(1)} %copy-done.3, f32[768]{0:T(1024)S(1)} %copy-done.9, f32[2048]{0:T(1024)S(1)} %add_rsqrt_fusion.1), kind=kLoop, calls=%fused_computation.15 | loop fusion | flops 6291456 | bytes 6302720 | tf_op jit(solution)/shard_map/convert_element_type | solution.py:59
  22.2 9.2 %all-to-all-start.1 = ((bf16[3,32,24,768]{3,2,0,1:T(8,128)(2,1)}), bf16[3,32,24,768]{3,2,0,1:T(8,128)(2,1)}, u32[]{:S(2)}, u32[]{:S(2)}) async-start(bf16[3,32,24,768]{3,2,0,1:T(8,128)(2,1)} %broadcast_in_dim.30), calls=%async_computation.1 | async-start | bytes 7077888 | tf_op jit(solution)/shard_map/all_to_all | solution.py:75
  34.5 2.7 %add_add_fusion = s32[1024,8,128]{0,1,2:T(8,128)S(1)} fusion(s32[1024,8,128]{0,1,2:T(8,128)} %copy-done.2, s32[1024,8]{0,1:T(8,128)S(1)} %slice.93), kind=kLoop, calls=%fused_computation.24 | loop fusion | flops 2097152 | bytes 8421376 | tf_op jit(solution)/shard_map/sub | solution.py:142
  37.2 2.4 %copy.100 = s32[1024,8,128]{0,2,1:T(8,128)S(1)} copy(s32[1024,8,128]{0,1,2:T(8,128)S(1)} %add_add_fusion) | data formatting | bytes 8388608 | tf_op jit(solution)/shard_map/sub | solution.py:142
  43.9 4.0 %fusion = pred[128,2048]{1,0:T(8,128)(4,1)S(1)} fusion(s32[128,8]{1,0:T(8,128)S(1)} %copy.102), kind=kLoop, calls=%fused_computation.8 | loop fusion | flops 3932160 | bytes 266240 | tf_op jit(solution)/shard_map/reduce_or | solution.py:145
  47.9 2.7 %convolution_convert_fusion = bf16[2048,768]{1,0:T(8,128)(2,1)} fusion(pred[128,2048]{1,0:T(8,128)(4,1)S(1)} %fusion, bf16[128,768]{1,0:T(8,128)(2,1)S(1)} %copy-done.7), kind=kOutput, calls=%fused_computation.31 | convolution fusion | flops 404226048 | bytes 3604480 | tf_op jit(solution)/shard_map/dot_general | solution.py:146
  50.6 8.6 %fusion.35 = f32[2048,768]{1,0:T(8,128)} fusion(bf16[768,768]{1,0:T(8,128)(2,1)S(1)} %copy-done, bf16[2048,768]{1,0:T(8,128)(2,1)} %fusion.5, bf16[768,768]{1,0:T(8,128)(2,1)S(1)} %copy-done.6), kind=kOutput, calls=%fused_computation.50 | convolution fusion | flops 4834983936 | bytes 11796480 | tf_op jit(solution)/shard_map/dot_general | solution.py:97
  59.2 16.1 %all-to-all-done.1 = bf16[3,32,24,768]{3,2,0,1:T(8,128)(2,1)} async-done(((bf16[3,32,24,768]{3,2,0,1:T(8,128)(2,1)}), bf16[3,32,24,768]{3,2,0,1:T(8,128)(2,1)}, u32[]{:S(2)}, u32[]{:S(2)}) %all-to-all-start.1) | async-done | bytes 3538976 | tf_op jit(solution)/shard_map/all_to_all | solution.py:75
  75.3 9.2 %all-to-all-start.3 = ((bf16[128,16,768]{2,1,0:T(8,128)(2,1)}), bf16[128,16,768]{2,1,0:T(8,128)(2,1)}, u32[]{:S(2)}, u32[]{:S(2)}) async-start(bf16[128,16,768]{2,1,0:T(8,128)(2,1)} %bitcast.66), calls=%async_computation.3 | async-start | bytes 6291456 | tf_op jit(solution)/shard_map/all_to_all | solution.py:149
  84.5 4.0 %copy.92 = bf16[3,32,24,768]{3,2,1,0:T(8,128)(2,1)} copy(bf16[3,32,24,768]{3,2,0,1:T(8,128)(2,1)} %all-to-all-done.1) | data formatting | bytes 7077888 | tf_op jit(solution)/shard_map/all_to_all | solution.py:75
  88.5 22.1 %multiply_reduce_fusion = (f32[2048]{0:T(1024)S(1)}, f32[2048,768]{1,0:T(8,128)}) fusion(f32[2048,768]{1,0:T(8,128)} %fusion.35, bf16[2304,768]{1,0:T(8,128)(2,1)} %bitcast.70, bf16[2048,768]{1,0:T(8,128)(2,1)} %fusion.5, s32[]{:T(128)S(6)} %select_n.56, bf16[768,3072]{1,0:T(8,128)(2,1)} %all-gather.2.cloned.1.call-done, bf16[2048,768]{1,0:T(8,128)(2,1)} %param.14), kind=kOutput, calls=%fused_computation.18 | convolution fusion | flops 14519891968 | bytes 27140100 | tf_op jit(solution)/shard_map/dot_general | solution.py:97
  110.7 3.8 %bitcast_reduce_fusion = f32[32,768]{1,0:T(8,128)S(1)} fusion(f32[2048,768]{1,0:T(8,128)} %get-tuple-element.43, f32[768]{0:T(1024)S(1)} %copy-done.10, f32[2048]{0:T(1024)S(1)} %add_rsqrt_fusion), kind=kLoop, calls=%fused_computation.16 | loop fusion | flops 4694016 | bytes 6401024 | tf_op jit(solution)/shard_map/reduce_sum | solution.py:102
  116.0 10.5 %all-to-all-done.3 = bf16[128,16,768]{2,1,0:T(8,128)(2,1)} async-done(((bf16[128,16,768]{2,1,0:T(8,128)(2,1)}), bf16[128,16,768]{2,1,0:T(8,128)(2,1)}, u32[]{:S(2)}, u32[]{:S(2)}) %all-to-all-start.3) | async-done | bytes 3145760 | tf_op jit(solution)/shard_map/all_to_all | solution.py:149
  126.4 3.8 %all-to-all-start.2 = ((bf16[128,2,896]{2,1,0:T(2,128)(2,1)}), bf16[128,2,896]{2,1,0:T(2,128)(2,1)S(1)}, u32[]{:S(2)}, u32[]{:S(2)}) async-start(bf16[128,2,896]{2,1,0:T(2,128)(2,1)} %all_to_all.30), calls=%async_computation.2 | async-start | bytes 917504 | tf_op jit(solution)/shard_map/all_to_all | solution.py:124
  130.2 4.6 %copy.103 = bf16[128,16,768]{2,0,1:T(8,128)(2,1)} copy(bf16[128,16,768]{2,1,0:T(8,128)(2,1)} %all-to-all-done.3) | data formatting | bytes 6291456 | tf_op jit(solution)/shard_map/all_to_all | solution.py:149
  134.8 8.7 %all-to-all-done.2 = bf16[128,2,896]{2,1,0:T(2,128)(2,1)S(1)} async-done(((bf16[128,2,896]{2,1,0:T(2,128)(2,1)}), bf16[128,2,896]{2,1,0:T(2,128)(2,1)S(1)}, u32[]{:S(2)}, u32[]{:S(2)}) %all-to-all-start.2) | async-done | bytes 458784 | tf_op jit(solution)/shard_map/all_to_all | solution.py:124
  151.2 6.5 %copy.109 = bf16[128,16,896]{2,1,0:T(8,128)(2,1)} copy(bf16[128,16,896]{0,2,1:T(8,128)(2,1)} %bitcast.65) | data formatting | bytes 7340032 | tf_op jit(solution)/shard_map/all_to_all | solution.py:164
  157.7 4.8 %all-to-all-start.4 = ((bf16[128,16,896]{2,1,0:T(8,128)(2,1)}), bf16[128,16,896]{2,1,0:T(8,128)(2,1)}, u32[]{:S(2)}, u32[]{:S(2)}) async-start(bf16[128,16,896]{2,1,0:T(8,128)(2,1)} %copy.109), calls=%async_computation.4 | async-start | bytes 7340032 | tf_op jit(solution)/shard_map/all_to_all | solution.py:164
  162.9 47.2 %all-to-all-done.4 = bf16[128,16,896]{2,1,0:T(8,128)(2,1)} async-done(((bf16[128,16,896]{2,1,0:T(8,128)(2,1)}), bf16[128,16,896]{2,1,0:T(8,128)(2,1)}, u32[]{:S(2)}, u32[]{:S(2)}) %all-to-all-start.4) | async-done | bytes 3670048 | tf_op jit(solution)/shard_map/all_to_all | solution.py:164
  210.1 2.9 %fusion.1 = f32[1024,128]{0,1:T(8,128)S(1)} fusion(s32[1024]{0:T(1024)S(1)} %multiply_add_fusion.1, bf16[2048,896]{1,0:T(8,128)(2,1)} %bitcast.17), kind=kOutput, calls=%fused_computation.10 | convolution fusion | flops 538968064 | bytes 1052672 | tf_op jit(solution)/shard_map/dot_general | solution.py:167
  213.5 2.8 %select_reduce_fusion = f32[128,2048]{1,0:T(8,128)S(1)} fusion(f32[128,8]{1,0:T(8,128)S(1)} %get-tuple-element.37, s32[128,8]{1,0:T(8,128)S(1)} %copy.102), kind=kLoop, calls=%fused_computation.6 | loop fusion | flops 6029312 | bytes 1056768 | tf_op jit(solution)/shard_map/reduce_sum | solution.py:185
  216.8 4.1 %fusion.31 = f32[128,768]{1,0:T(8,128)} fusion(f32[128,768]{1,0:T(8,128)S(1)} %get-tuple-element.45, f32[128,2048]{1,0:T(8,128)S(1)} %select_reduce_fusion, bf16[2048,896]{1,0:T(8,128)(2,1)} %bitcast.17, f32[128]{0:T(128)S(1)} %get-tuple-element.34, f32[128]{0:T(128)S(1)} %get-tuple-element.35), kind=kOutput, calls=%fused_computation.46 | convolution fusion | flops 2416410624 | bytes 4981760 | tf_op jit(solution)/shard_map/dot_general | solution.py:192
  (88 shorter events, 22.6 us)
Async XLA Ops:
  7.2 1.3 copy-start
  7.2 10.5 %copy-start.9 = (f32[768]{0:T(1024)S(1)}, f32[768]{0:T(1024)}, u32[]{:S(2)}) copy-start(f32[768]{0:T(1024)} %param.17) | copy-start | bytes 9220
  7.2 81.3 %all-gather.2.cloned.1.call-start = ((), (), s32[]{:S(2)}) async-start(), calls=%async_computation.5 | async-start | bytes 5898240 | tf_op jit(solution)/shard_map/all_gather | solution.py:83
  9.1 11.0 %all-to-all-start = ((bf16[4,24,768]{2,1,0:T(8,128)(2,1)}), bf16[4,24,768]{2,1,0:T(8,128)(2,1)S(1)}, u32[]{:S(2)}, u32[]{:S(2)}) async-start(bf16[4,24,768]{2,1,0:T(8,128)(2,1)} %broadcast_in_dim.29), calls=%async_computation | async-start | bytes 294912 | tf_op jit(solution)/shard_map/all_to_all | solution.py:65
  14.7 2.9 %copy-start.3 = (bf16[2048,768]{1,0:T(8,128)(2,1)S(1)}, bf16[2048,768]{1,0:T(8,128)(2,1)}, u32[]{:S(2)}) copy-start(bf16[2048,768]{1,0:T(8,128)(2,1)} %param.14) | copy-start | bytes 9437188
  22.2 9.3 %copy-start.8 = (s32[128,8]{0,1:T(8,128)S(1)}, s32[128,8]{0,1:T(8,128)}, u32[]{:S(2)}) copy-start(s32[128,8]{0,1:T(8,128)} %param.22) | copy-start | bytes 12292
  22.2 53.2 %all-to-all-start.1 = ((bf16[3,32,24,768]{3,2,0,1:T(8,128)(2,1)}), bf16[3,32,24,768]{3,2,0,1:T(8,128)(2,1)}, u32[]{:S(2)}, u32[]{:S(2)}) async-start(bf16[3,32,24,768]{3,2,0,1:T(8,128)(2,1)} %broadcast_in_dim.30), calls=%async_computation.1 | async-start | bytes 7077888 | tf_op jit(solution)/shard_map/all_to_all | solution.py:75
  32.5 1.9 copy-start.2
  39.7 8.2 %copy-start.7 = (bf16[128,768]{1,0:T(8,128)(2,1)S(1)}, bf16[128,768]{1,0:T(8,128)(2,1)}, u32[]{:S(2)}) copy-start(bf16[128,768]{1,0:T(8,128)(2,1)} %param.21) | copy-start | bytes 589828
  39.7 10.9 %copy-start.6 = (bf16[768,768]{1,0:T(8,128)(2,1)S(1)}, bf16[768,768]{1,0:T(8,128)(2,1)}, u32[]{:S(2)}) copy-start(bf16[768,768]{1,0:T(8,128)(2,1)} %param.15) | copy-start | bytes 3538948
  75.3 51.1 %all-to-all-start.3 = ((bf16[128,16,768]{2,1,0:T(8,128)(2,1)}), bf16[128,16,768]{2,1,0:T(8,128)(2,1)}, u32[]{:S(2)}, u32[]{:S(2)}) async-start(bf16[128,16,768]{2,1,0:T(8,128)(2,1)} %bitcast.66), calls=%async_computation.3 | async-start | bytes 6291456 | tf_op jit(solution)/shard_map/all_to_all | solution.py:149
  88.5 22.1 %copy-start.10 = (f32[768]{0:T(1024)S(1)}, f32[768]{0:T(1024)}, u32[]{:S(2)}) copy-start(f32[768]{0:T(1024)} %param.18) | copy-start | bytes 9220
  126.4 17.1 %all-to-all-start.2 = ((bf16[128,2,896]{2,1,0:T(2,128)(2,1)}), bf16[128,2,896]{2,1,0:T(2,128)(2,1)S(1)}, u32[]{:S(2)}, u32[]{:S(2)}) async-start(bf16[128,2,896]{2,1,0:T(2,128)(2,1)} %all_to_all.30), calls=%async_computation.2 | async-start | bytes 917504 | tf_op jit(solution)/shard_map/all_to_all | solution.py:124
  143.7 2.7 %copy-start.4 = (bf16[128,16,768]{2,0,1:T(8,128)(2,1)S(1)}, bf16[128,16,768]{2,0,1:T(8,128)(2,1)}, u32[]{:S(2)}) copy-start(bf16[128,16,768]{2,0,1:T(8,128)(2,1)} %copy.103) | copy-start | bytes 9437188
  146.4 2.2 copy-start.5
  157.7 4.8 %copy-start.11 = (s32[128]{0:T(128)S(1)}, s32[128]{0:T(128)}, u32[]{:S(2)}) copy-start(s32[128]{0:T(128)} %param.23) | copy-start | bytes 1540
  157.7 52.4 %all-to-all-start.4 = ((bf16[128,16,896]{2,1,0:T(8,128)(2,1)}), bf16[128,16,896]{2,1,0:T(8,128)(2,1)}, u32[]{:S(2)}, u32[]{:S(2)}) async-start(bf16[128,16,896]{2,1,0:T(8,128)(2,1)} %copy.109), calls=%async_computation.4 | async-start | bytes 7340032 | tf_op jit(solution)/shard_map/all_to_all | solution.py:164
  213.3 7.6 %copy-start.1 = (bf16[768,768]{1,0:T(8,128)(2,1)S(1)}, bf16[768,768]{1,0:T(8,128)(2,1)}, u32[]{:S(2)}) copy-start(bf16[768,768]{1,0:T(8,128)(2,1)} %param.16) | copy-start | bytes 3538948
Sparse Core Ops, SparseCore 0:
  9.7 55.5 all-gather.1
